TPU v7x, 32 devices: a whole 2x2x4 slice. The times are simulated.
32 devices in a mesh: grp: 4 (over x, core), seg: 4 (over z), mp: 2 (over y).
Axes of the slice: x: 2, y: 2, z: 4, core: 2. Of those that a mesh axis runs over, the one named last changes fastest.
Arguments:
- tokens: bfloat16 [4096, 4096], P(('grp', 'seg'), 'mp'), may hold values from -6 to 6
- x_weight: bfloat16 [4096, 4096], P(('grp', 'seg'), 'mp'), may hold values from -0.09375 to 0.09375
- y_weight: bfloat16 [4096, 4096], P(('grp', 'seg'), 'mp'), may hold values from -0.09375 to 0.09375
- out_weight: bfloat16 [4096, 4096], P('mp', ('grp', 'seg')), may hold values from -0.09375 to 0.09375
- conv_weight: float32 [4, 4096], P(None, 'mp'), may hold values from -3 to 3
- conv_bias: float32 [4096], P('mp'), may hold values from -3 to 3
- decay_gate: bfloat16 [16, 256, 256], P('mp'), may hold values from -0.375 to 0.375
- decay_bias: float32 [4096], P('mp'), may hold values from -4 to 4
- input_gate: bfloat16 [16, 256, 256], P('mp'), may hold values from -0.375 to 0.375
- input_bias: float32 [4096], P('mp'), may hold values from -4 to 4
- log_rate: float32 [4096], P('mp'), may hold values from -19 to -5, as said below
- phase: float32 [4096], P('mp'), may hold values from -3.140625 to 3.140625
Outputs:
- mixed: bfloat16 [4096, 4096], P(('grp', 'seg'), 'mp')
Inputs may be any that keep to these rules, and one draw needn't show every extreme that they name: softplus(log_rate) lies between 1e-8 and 1e-2.
All inputs are finite; a program needn't handle non-finite values.
Results may differ from a plain program's by a relative error of at most 0.015.
Values may be sent and summed in bfloat16 or wider, within the bound.
No kernel may reach another device: no remote copies, remote signals or barrier semaphores. Data moves between devices by JAX's collectives and lax.ppermute only.
A program may use at most 128 MiB of HBM per device.

v0:
```python
import jax
import jax.numpy as jnp
from jax import lax
from jax.experimental import pallas as pl
from jax.experimental.pallas import tpu as pltpu
from jax.sharding import PartitionSpec as P


VMEM = pl.BlockSpec(memory_space=pltpu.VMEM)
SMEM = pl.BlockSpec(memory_space=pltpu.SMEM)
GRANT = 56 * 1024 * 1024


def shifted(value, axis, by):
    peers = lax.axis_size(axis)
    pairs = [(i, i + by) for i in range(peers) if 0 <= i + by < peers]
    return lax.ppermute(value, axis, pairs)


def carried_in(value, axis, join, neutral):
    count, mine = (lax.axis_size(axis), lax.axis_index(axis))
    pieces = lax.all_gather(value, axis)
    total = jnp.full_like(value, 0) + jnp.asarray(neutral, value.dtype)

    def turn(position, total):
        longer = join(total, pieces[position])
        return jnp.where(position < mine, longer, total)

    return lax.fori_loop(0, count - 1, turn, total)


def combine(earlier, later):
    first_real = earlier[0] * later[0] - earlier[1] * later[1]
    first_imag = earlier[0] * later[1] + earlier[1] * later[0]
    state_real = later[0] * earlier[2] - later[1] * earlier[3] + later[2]
    state_imag = later[0] * earlier[3] + later[1] * earlier[2] + later[3]
    return jnp.stack([first_real, first_imag, state_real, state_imag])


def neutral(count):
    ones_row = jnp.ones((count,), jnp.float32)
    zeros_row = jnp.zeros((count,), jnp.float32)
    return jnp.stack([ones_row, zeros_row, zeros_row, zeros_row])


def general(
    tokens,
    x_weight,
    y_weight,
    out_weight,
    conv_weight,
    conv_bias,
    decay_gate,
    decay_bias,
    input_gate,
    input_bias,
    log_rate,
    phase,
):
    source = lax.all_gather(tokens, "mp", axis=1, tiled=True)
    tokens_here = source.shape[0]
    width = x_weight.shape[1]

    def add_rows(shard_piece):
        return jnp.dot(source, shard_piece, preferred_element_type=jnp.float32)

    x_sum = add_rows(lax.all_gather(x_weight, ("grp", "seg"), axis=0, tiled=True))
    y_sum = add_rows(lax.all_gather(y_weight, ("grp", "seg"), axis=0, tiled=True))
    x_proj = x_sum.astype(jnp.bfloat16)
    branch = jax.nn.gelu(y_sum)
    taps = conv_weight.shape[0]
    last_rows = x_proj[tokens_here - (taps - 1) :]
    before = shifted(last_rows, ("grp", "seg"), 1)
    padded = jnp.concatenate([before, x_proj], axis=0).astype(jnp.float32)
    convolved = conv_bias + jnp.zeros((tokens_here, width), jnp.float32)
    for offset in range(taps):
        convolved = (
            convolved
            + conv_weight[offset] * padded[taps - 1 - offset : taps - 1 - offset + tokens_here]
        )
    convolved = convolved.astype(jnp.bfloat16)
    heads_here = decay_gate.shape[0]
    block_size = decay_gate.shape[1]
    head_view = convolved.reshape(tokens_here, heads_here, block_size)
    rate_gate = jax.nn.sigmoid(
        jnp.einsum(
            "nhd,hde->nhe", head_view, decay_gate, preferred_element_type=jnp.float32
        ).reshape(tokens_here, width)
        + decay_bias
    )
    input_open = jax.nn.sigmoid(
        jnp.einsum(
            "nhd,hde->nhe", head_view, input_gate, preferred_element_type=jnp.float32
        ).reshape(tokens_here, width)
        + input_bias
    )
    log_decay = -8.0 * rate_gate * jax.nn.softplus(log_rate)
    decay = jnp.exp(log_decay)
    drive = jnp.sqrt(-jnp.expm1(2.0 * log_decay)) * input_open * convolved.astype(jnp.float32)
    elements = jnp.stack(
        [decay * jnp.cos(phase), decay * jnp.sin(phase), drive, jnp.zeros_like(drive)]
    )
    running = lax.associative_scan(combine, elements, axis=1)
    summary = running[:, tokens_here - 1]
    identity = neutral(width)
    carry_in = carried_in(summary, ("grp", "seg"), combine, identity)
    state_real = running[2] + running[0] * carry_in[2] - running[1] * carry_in[3]
    gated = (branch * state_real).astype(jnp.bfloat16)
    partial_value = jnp.dot(
        gated,
        lax.all_gather(out_weight, ("grp", "seg"), axis=1, tiled=True),
        preferred_element_type=jnp.float32,
    )
    reduced = lax.psum_scatter(
        partial_value.astype(jnp.bfloat16), "mp", scatter_dimension=1, tiled=True
    )
    return reduced


def swap(value, axis, bit):
    count = lax.axis_size(axis)
    return lax.ppermute(value, axis, [(i, i ^ bit) for i in range(count)])


def spread(own, other):
    near = [own]
    for b in range(1, lax.axis_size("seg")):
        near.append(swap(other if b % 2 else own, "seg", b))
    return near, [swap(piece, "grp", 2) for piece in near]


def assemble(place, pieces, segs):
    rows, wide = pieces[0].shape
    lows = len(pieces) // 4
    block = wide // 2 // segs

    def kernel(place_ref, *refs):
        c, z, turn, low = place_ref[0], place_ref[1], place_ref[2], place_ref[6]
        for b in range(segs):
            for d in range(2):
                source = pl.multiple_of(((c ^ d) * segs + (z ^ b)) * block, block)
                for index, piece in enumerate(refs[:-1]):
                    e, f, h = index // (2 * lows), index // 2 % lows, index % 2
                    at_low = low ^ f if lows == 2 else 0
                    row = pl.multiple_of(((c ^ e) * lows + at_low) * rows, rows)
                    column = pl.multiple_of((turn ^ h) * wide + (b * 2 + d) * block, block)
                    refs[-1][pl.ds(row, rows), pl.ds(column, block)] = piece[
                        :, pl.ds(source, block)
                    ]

    return pl.pallas_call(
        kernel,
        out_shape=jax.ShapeDtypeStruct((2 * lows * rows, 2 * wide), pieces[0].dtype),
        in_specs=[SMEM] + [VMEM] * len(pieces),
        out_specs=VMEM,
        compiler_params=pltpu.CompilerParams(vmem_limit_bytes=GRANT),
        cost_estimate=pl.CostEstimate(
            flops=0, bytes_accessed=4 * len(pieces) * rows * wide, transcendentals=0
        ),
        name="set_together",
    )(place, *pieces)


def matmul_sum(source, pieces):
    deep = pieces[0].shape[0]
    total = None
    for index, piece in enumerate(pieces):
        term = jnp.dot(
            source[:, index * deep : (index + 1) * deep],
            piece[...],
            preferred_element_type=jnp.float32,
        )
        total = term if total is None else total + term
    return total


def project(source, half, pieces, edge=None, before=None, state=None, last=True, rows=256):
    tokens_here = source.shape[0]
    depth = source.shape[1] // 2
    width = pieces[0].shape[1]
    count = len(pieces)
    kind = jnp.bfloat16 if last else jnp.float32

    def row_block(i):
        return (i, 0)

    def whole(i):
        return (0, 0)

    specs = [pl.BlockSpec((rows, depth), lambda i: (i, half))]
    specs += [pl.BlockSpec(p.shape, whole) for p in pieces]
    operands = [source, *pieces]
    out_specs = [pl.BlockSpec((rows, width), row_block)]
    out_shape = [jax.ShapeDtypeStruct((tokens_here, width), kind)]
    if before is not None:
        specs.append(pl.BlockSpec((rows, width), row_block))
        operands.append(before)
    if state is not None:
        specs.append(pl.BlockSpec((width // LANES, rows, LANES), lambda i: (0, i, 0)))
        operands.append(state)
    if edge is not None:
        short, others = edge
        specs += [pl.BlockSpec(a.shape, whole) for a in (short, *others)]
        operands += [short, *others]
        out_specs.append(pl.BlockSpec((short.shape[0], width), whole))
        out_shape.append(jax.ShapeDtypeStruct((short.shape[0], width), kind))
    outs = len(out_shape)

    def kernel(source_ref, *refs):
        weights, extra, out = refs[:count], list(refs[count:-outs]), refs[-outs:]
        total = matmul_sum(source_ref, weights)
        if before is not None:
            total = total + extra.pop(0)[...]
        if state is not None:
            state_ref = extra.pop(0)
            slabs = [state_ref[j] for j in range(width // LANES)]
            total = jax.nn.gelu(total) * jnp.concatenate(slabs, axis=1)
        out[0][...] = total.astype(kind)
        if edge is not None:

            @pl.when(pl.program_id(0) == 0)
            def edge_rows():
                short_ref = extra[0]
                halves = [short_ref.at[:, k * depth : (k + 1) * depth] for k in range(2)]
                ends = matmul_sum(halves[half], weights) + matmul_sum(halves[1 - half], extra[1:])
                out[1][...] = ends.astype(kind)

    return pl.pallas_call(
        kernel,
        grid=(tokens_here // rows,),
        out_shape=out_shape,
        in_specs=specs,
        out_specs=out_specs,
        compiler_params=pltpu.CompilerParams(vmem_limit_bytes=GRANT),
        cost_estimate=pl.CostEstimate(
            flops=2 * tokens_here * depth * width,
            bytes_accessed=2 * (tokens_here * depth + depth * width),
            transcendentals=0,
        ),
        name="project",
    )(*operands)


SUBS = 8
LANES = 128


def advance(decay, drive, cosine, sine, real, imag):
    return (
        decay * (cosine * real - sine * imag) + drive,
        decay * (sine * real + cosine * imag),
    )


def expm1(value):
    near = 1.0 + value * (1.0 / 9.0)
    for k in range(8, 1, -1):
        near = 1.0 + (value * (1.0 / k)) * near
    return jnp.where(value > -0.5, value * near, jnp.exp(value) - 1.0)


def spread_lanes(table_ref, row):
    size = table_ref.shape[1]
    return [
        jnp.broadcast_to(table_ref[row : row + 1, j : j + LANES], (SUBS, LANES))
        for j in range(0, size, LANES)
    ]


def decay_and_drive(convolved, decay_w, input_w, table_ref, taps):
    convolved = convolved.astype(jnp.bfloat16)
    rate = jax.nn.sigmoid(
        jnp.dot(convolved, decay_w[0], preferred_element_type=jnp.float32)
        + table_ref[taps + 1 : taps + 2, :]
    )
    opened = jax.nn.sigmoid(
        jnp.dot(convolved, input_w[0], preferred_element_type=jnp.float32)
        + table_ref[taps + 2 : taps + 3, :]
    )
    log_decay = rate * table_ref[taps + 3 : taps + 4, :]
    drive = jnp.sqrt(-expm1(2.0 * log_decay)) * opened * convolved.astype(jnp.float32)
    return jnp.exp(log_decay), drive


def run_gates(place, x_proj, table, decay_gate, input_gate, taps):
    tokens_here, width = x_proj.shape
    size = decay_gate.shape[1]
    heads = width // size
    length = tokens_here // 2
    part = length // SUBS

    def kernel(
        place_ref, x_ref, table_ref, decay_w, input_w,
        decay_ref, drive_ref, part_ref, total_ref, padded,
    ):
        padded[0:8, :] = jnp.zeros((8, size), jnp.float32)
        padded[8 : 8 + length, :] = x_ref[...].astype(jnp.float32)
        convolved = table_ref[taps : taps + 1, :] + jnp.zeros((length, size), jnp.float32)
        for k in range(taps):
            convolved = convolved + table_ref[k : k + 1, :] * padded[8 - k : 8 - k + length, :]
        decay, drive = decay_and_drive(convolved, decay_w, input_w, table_ref, taps)
        for j in range(size // LANES):
            decay_ref[j] = decay[:, j * LANES : (j + 1) * LANES]
            drive_ref[j] = drive[:, j * LANES : (j + 1) * LANES]
            decay_ref[j, 0 : taps - 1, :] = jnp.ones((taps - 1, LANES), jnp.float32)
            drive_ref[j, 0 : taps - 1, :] = jnp.zeros((taps - 1, LANES), jnp.float32)
        cosines = spread_lanes(table_ref, taps + 4)
        sines = spread_lanes(table_ref, taps + 5)

        def step(t, carry):
            after = []
            for j, (real, imag, product) in enumerate(carry):
                here = decay_ref[j, pl.ds(t, SUBS, stride=part), :]
                push = drive_ref[j, pl.ds(t, SUBS, stride=part), :]
                real, imag = advance(here, push, cosines[j], sines[j], real, imag)
                after.append((real, imag, product * here))
            return tuple(after)

        zeros = jnp.zeros((SUBS, LANES), jnp.float32)
        ends = lax.fori_loop(
            0, part, step, ((zeros, zeros, zeros + 1.0),) * (size // LANES), unroll=8
        )
        real, imag, product = (jnp.concatenate(rows, axis=1) for rows in zip(*ends))
        part_ref[0, 0:SUBS, :] = real
        part_ref[0, SUBS : 2 * SUBS, :] = imag
        part_ref[0, 2 * SUBS : 3 * SUBS, :] = product
        turn_cos, turn_sin = table_ref[taps + 6 : taps + 7, :], table_ref[taps + 7 : taps + 8, :]
        end_real, end_imag = real[0:1], imag[0:1]
        whole = product[0:1]
        for j in range(1, SUBS):
            here = product[j : j + 1]
            end_real, end_imag = (
                here * (turn_cos * end_real - turn_sin * end_imag) + real[j : j + 1],
                here * (turn_sin * end_real + turn_cos * end_imag) + imag[j : j + 1],
            )
            whole = whole * here
        total_ref[0, 0:1, :] = end_real
        total_ref[0, 1:2, :] = end_imag
        total_ref[0, 2:3, :] = whole
        total_ref[0, 3:8, :] = padded[8:13, :]
        total_ref[0, 8:16, :] = padded[length : length + 8, :]

    depth = table.shape[0]
    grid_spec = pltpu.PrefetchScalarGridSpec(
        num_scalar_prefetch=1,
        grid=(heads, 2),
        in_specs=[
            pl.BlockSpec((length, size), lambda h, r, p: (r, h)),
            pl.BlockSpec((depth, size), lambda h, r, p: (0, p[4] * heads + h)),
            pl.BlockSpec((1, size, size), lambda h, r, p: (p[4] * heads + h, 0, 0)),
            pl.BlockSpec((1, size, size), lambda h, r, p: (p[4] * heads + h, 0, 0)),
        ],
        out_specs=[
            pl.BlockSpec((size // LANES, length, LANES), lambda h, r, p: (h, r, 0)),
            pl.BlockSpec((size // LANES, length, LANES), lambda h, r, p: (h, r, 0)),
            pl.BlockSpec((1, 3 * SUBS, size), lambda h, r, p: (r, 0, h)),
            pl.BlockSpec((1, 16, size), lambda h, r, p: (r, 0, h)),
        ],
        scratch_shapes=[pltpu.VMEM((length + 8, size), jnp.float32)],
    )
    return pl.pallas_call(
        kernel,
        grid_spec=grid_spec,
        out_shape=[
            jax.ShapeDtypeStruct((width // LANES, tokens_here, LANES), jnp.float32),
            jax.ShapeDtypeStruct((width // LANES, tokens_here, LANES), jnp.float32),
            jax.ShapeDtypeStruct((2, 3 * SUBS, width), jnp.float32),
            jax.ShapeDtypeStruct((2, 16, width), jnp.float32),
        ],
        compiler_params=pltpu.CompilerParams(vmem_limit_bytes=GRANT),
        cost_estimate=pl.CostEstimate(
            flops=4 * tokens_here * width * size,
            bytes_accessed=10 * tokens_here * width,
            transcendentals=8 * tokens_here * width,
        ),
        name="gates",
    )(place, x_proj, table, decay_gate, input_gate)


def run_states(
    place, decay, drive, parts, totals, table, decay_gate, input_gate, taps, outer, highs
):
    tokens_here, width = decay.shape[1], decay.shape[0] * LANES
    size = decay_gate.shape[1]
    heads = width // size
    length = tokens_here // 2
    part = length // SUBS
    first = taps - 1
    runs = outer * 2 * highs

    def kernel(
        place_ref, decay_ref, drive_ref, part_ref, total_ref, table_ref, decay_w, input_w,
        state_ref, starts, begin, rows_ref, early_decay, early_drive,
    ):
        x, high = place_ref[3], place_ref[5]
        run = pl.program_id(1)

        def row(k):
            return table_ref[taps + k : taps + k + 1, :]

        def turned(here, cosine, sine, real, imag, add_real, add_imag):
            return (
                here * (cosine * real - sine * imag) + add_real,
                here * (sine * real + cosine * imag) + add_imag,
            )

        def begun(base, real, imag):
            here, push = early_decay[pl.ds(base, 8), :], early_drive[pl.ds(base, 8), :]
            for t in range(first):
                real, imag = turned(
                    here[t : t + 1], row(4), row(5), real, imag, push[t : t + 1], 0.0
                )
            return real, imag

        def slot(q):
            at_x, at_run, at_high = q // (2 * highs), q // highs % 2, q % highs
            return ((x ^ at_x) * highs + (high ^ at_high)) * 2 + at_run

        @pl.when(run == 0)
        def every_run():
            zeros = jnp.zeros((8, size), jnp.float32)
            for q in range(runs):
                mine = total_ref[slot(q)]
                if q == 0:
                    rows_ref[0:8, :] = zeros
                else:
                    rows_ref[0:8, :] = total_ref[slot(q - 1)][8:16]
                rows_ref[8:16, :] = zeros
                rows_ref[8 : 8 + first, :] = mine[3 : 3 + first]
                convolved = row(0) + zeros
                for k in range(taps):
                    convolved = convolved + table_ref[k : k + 1, :] * rows_ref[8 - k : 16 - k, :]
                early_drive[q * 8 : q * 8 + 8, :] = convolved
            here, push = decay_and_drive(early_drive[...], decay_w, input_w, table_ref, taps)
            early_decay[...] = here
            early_drive[...] = push
            real = jnp.zeros((1, size), jnp.float32)
            imag = jnp.zeros((1, size), jnp.float32)
            for q in range(runs):
                at_run = q // highs % 2
                ours = (x == q // (2 * highs)) & (high == q % highs)

                @pl.when(ours)
                def keep():
                    begin[8 * at_run : 8 * at_run + 1, :] = real
                    begin[8 * at_run + 1 : 8 * at_run + 2, :] = imag

                if q < runs - 1:
                    mine = total_ref[slot(q)]
                    real, imag = begun(q * 8, real, imag)
                    real, imag = turned(
                        mine[2:3], row(8), row(9), real, imag, mine[0:1], mine[1:2]
                    )

        base = pl.multiple_of(((x * 2 + run) * highs + high) * 8, 8)
        kept = begin[pl.ds(pl.multiple_of(run * 8, 8), 8), :]
        real, imag = kept[0:1], kept[1:2]
        early_here, early_push = early_decay[pl.ds(base, 8), :], early_drive[pl.ds(base, 8), :]
        for j in range(SUBS):
            starts[j : j + 1, :] = real
            starts[SUBS + j : SUBS + j + 1, :] = imag
            if j == 0:
                real, imag = begun(base, real, imag)
            spin = row(10), row(11)
            if j > 0:
                spin = row(6), row(7)
            real, imag = turned(
                part_ref[0, 2 * SUBS + j : 2 * SUBS + j + 1, :], *spin, real, imag,
                part_ref[0, j : j + 1, :], part_ref[0, SUBS + j : SUBS + j + 1, :],
            )
        cosines = spread_lanes(table_ref, taps + 4)
        sines = spread_lanes(table_ref, taps + 5)
        top = lax.broadcasted_iota(jnp.int32, (SUBS, LANES), 0) == 0

        def step(t, carry, early=False):
            after = []
            for j, (real, imag) in enumerate(carry):
                here = decay_ref[j, pl.ds(t, SUBS, stride=part), :]
                push = drive_ref[j, pl.ds(t, SUBS, stride=part), :]
                if early:
                    lanes = slice(j * LANES, (j + 1) * LANES)
                    here = jnp.where(top, early_here[t : t + 1, lanes], here)
                    push = jnp.where(top, early_push[t : t + 1, lanes], push)
                real, imag = advance(here, push, cosines[j], sines[j], real, imag)
                state_ref[j, pl.ds(t, SUBS, stride=part), :] = real
                after.append((real, imag))
            return tuple(after)

        carry = tuple(
            (starts[0:SUBS, j : j + LANES], starts[SUBS : 2 * SUBS, j : j + LANES])
            for j in range(0, size, LANES)
        )
        for t in range(8):
            carry = step(t, carry, t < first)
        lax.fori_loop(8, part, step, carry, unroll=8)

    depth = table.shape[0]
    slots = totals.shape[0]
    grid_spec = pltpu.PrefetchScalarGridSpec(
        num_scalar_prefetch=1,
        grid=(heads, 2),
        in_specs=[
            pl.BlockSpec((size // LANES, length, LANES), lambda h, r, p: (h, r, 0)),
            pl.BlockSpec((size // LANES, length, LANES), lambda h, r, p: (h, r, 0)),
            pl.BlockSpec((1, 3 * SUBS, size), lambda h, r, p: (r, 0, h)),
            pl.BlockSpec((slots, 16, size), lambda h, r, p: (0, 0, h)),
            pl.BlockSpec((depth, size), lambda h, r, p: (0, p[4] * heads + h)),
            pl.BlockSpec((1, size, size), lambda h, r, p: (p[4] * heads + h, 0, 0)),
            pl.BlockSpec((1, size, size), lambda h, r, p: (p[4] * heads + h, 0, 0)),
        ],
        out_specs=pl.BlockSpec((size // LANES, length, LANES), lambda h, r, p: (h, r, 0)),
        scratch_shapes=[
            pltpu.VMEM((2 * SUBS, size), jnp.float32),
            pltpu.VMEM((16, size), jnp.float32),
            pltpu.VMEM((16, size), jnp.float32),
            pltpu.VMEM((runs * 8, size), jnp.float32),
            pltpu.VMEM((runs * 8, size), jnp.float32),
        ],
    )
    return pl.pallas_call(
        kernel,
        grid_spec=grid_spec,
        out_shape=jax.ShapeDtypeStruct((width // LANES, tokens_here, LANES), jnp.float32),
        compiler_params=pltpu.CompilerParams(vmem_limit_bytes=GRANT),
        cost_estimate=pl.CostEstimate(
            flops=10 * tokens_here * width,
            bytes_accessed=12 * tokens_here * width,
            transcendentals=0,
        ),
        name="states",
    )(place, decay, drive, parts, totals, table, decay_gate, input_gate)


def products(c, gated, weights):
    deep = gated[0].shape[1]
    spots = [pl.multiple_of((c ^ e) * deep, deep) for e in range(2)]
    blocks = []
    for weight in weights:
        terms = [
            jnp.dot(
                gated[e][...], weight[pl.ds(spots[e], deep), :], preferred_element_type=jnp.float32
            )
            for e in range(2)
        ]
        blocks.append(terms[0] + terms[1])
    return blocks


def mix_near(place, parts, pieces):
    tokens_here, deep = parts[0].shape
    width = pieces[0].shape[1]
    rows = tokens_here // 4
    count = len(pieces)

    def kernel(place_ref, *refs):
        blocks = products(place_ref[0], refs[:2], refs[2:-1])
        for b in range(count):
            refs[-1][:, b * width : (b + 1) * width] = blocks[b]

    return pl.pallas_call(
        kernel,
        grid=(4,),
        out_shape=jax.ShapeDtypeStruct((tokens_here, count * width), jnp.float32),
        in_specs=[SMEM]
        + [pl.BlockSpec((rows, deep), lambda i: (i, 0))] * 2
        + [pl.BlockSpec(piece.shape, lambda i: (0, 0)) for piece in pieces],
        out_specs=pl.BlockSpec((rows, count * width), lambda i: (i, 0)),
        compiler_params=pltpu.CompilerParams(vmem_limit_bytes=GRANT),
        cost_estimate=pl.CostEstimate(
            flops=4 * count * tokens_here * deep * width,
            bytes_accessed=4 * tokens_here * deep + 16 * count * rows * width,
            transcendentals=0,
        ),
        name="mix_near",
    )(place, *parts, *pieces)


def mix_far(place, parts, pieces, near, column):
    tokens_here, deep = parts[0].shape
    width = pieces[0].shape[1]
    rows = tokens_here // 4
    count = len(pieces)

    def kernel(place_ref, *refs):
        near_ref, leave_ref, stay_ref = refs[-3:]
        blocks = products(place_ref[0], refs[:2], refs[2:-3])
        blocks = [
            block + near_ref[:, b * width : (b + 1) * width] for b, block in enumerate(blocks)
        ]

        @pl.when(pl.program_id(1) == 0)
        def leave():
            for b in range(count):
                at = (count - 1 - b) * width
                leave_ref[:, at : at + width] = blocks[b].astype(jnp.bfloat16)

        @pl.when(pl.program_id(1) == 1)
        def stay():
            for b in range(count):
                stay_ref[:, b * width : (b + 1) * width] = blocks[b]

    def row(r, f, p):
        return r * 2 + (1 - f ^ p[6])

    grid_spec = pltpu.PrefetchScalarGridSpec(
        num_scalar_prefetch=1,
        grid=(2, 2),
        in_specs=[pl.BlockSpec((rows, deep), lambda r, f, p: (row(r, f, p), 0)) for _ in parts]
        + [pl.BlockSpec(piece.shape, lambda r, f, p: (0, 0)) for piece in pieces]
        + [pl.BlockSpec((rows, count * width), lambda r, f, p: (row(r, f, p), column))],
        out_specs=[pl.BlockSpec((rows, count * width), lambda r, f, p: (r, 0))] * 2,
    )
    return pl.pallas_call(
        kernel,
        grid_spec=grid_spec,
        out_shape=[
            jax.ShapeDtypeStruct((2 * rows, count * width), jnp.bfloat16),
            jax.ShapeDtypeStruct((2 * rows, count * width), jnp.float32),
        ],
        compiler_params=pltpu.CompilerParams(vmem_limit_bytes=GRANT),
        cost_estimate=pl.CostEstimate(
            flops=4 * count * tokens_here * deep * width,
            bytes_accessed=4 * tokens_here * deep + 28 * count * rows * width,
            transcendentals=0,
        ),
        name="mix_far",
    )(place, *parts, *pieces, near)


def place_columns(place, groups, own, other, block):
    rows = own[0].shape[0]
    segs = sum(len(group) for group in groups)

    def kernel(place_ref, *refs):
        c, z = place_ref[0], place_ref[1]
        whole = refs[-1]
        for i, group in enumerate(groups):
            for j, b in enumerate(group):
                for d in range(2):
                    at = pl.multiple_of(((c ^ d) * segs + (z ^ b)) * block, block)
                    from_ref = refs[d * len(groups) + i]
                    whole[:, pl.ds(at, block)] = from_ref[:, j * block : (j + 1) * block]

    return pl.pallas_call(
        kernel,
        out_shape=jax.ShapeDtypeStruct((rows, 2 * segs * block), own[0].dtype),
        in_specs=[SMEM] + [VMEM] * (2 * len(own)),
        out_specs=VMEM,
        name="place",
    )(place, *own, *other)


def folded(
    tokens,
    x_weight,
    y_weight,
    out_weight,
    conv_weight,
    conv_bias,
    decay_gate,
    decay_bias,
    input_gate,
    input_bias,
    log_rate,
    phase,
):
    grps, segs = lax.axis_size("grp"), lax.axis_size("seg")
    g, z, y = lax.axis_index("grp"), lax.axis_index("seg"), lax.axis_index("mp")
    outer, highs = grps // 2, segs // 2
    x, c = g // 2, g % 2
    high, low = z // 2, z % 2
    turn = x ^ y
    rows, _ = tokens.shape
    columns = x_weight.shape[1]
    width = columns // 4
    taps = conv_weight.shape[0]
    length = 2 * rows
    place = jnp.stack([c, z, turn, x, low * 2 + c, high, low]).astype(jnp.int32)

    part = length // SUBS

    def less(count):
        c_all, s_all = jnp.cos(count * phase), jnp.sin(count * phase)
        c_few, s_few = jnp.cos((taps - 1) * phase), jnp.sin((taps - 1) * phase)
        return c_all * c_few + s_all * s_few, s_all * c_few - c_all * s_few

    table = jnp.stack(
        [conv_weight[k] for k in range(taps)]
        + [
            conv_bias,
            decay_bias,
            input_bias,
            -8.0 * jax.nn.softplus(log_rate),
            jnp.cos(phase),
            jnp.sin(phase),
            jnp.cos(part * phase),
            jnp.sin(part * phase),
            *less(length),
            *less(part),
        ]
    )

    by_z = swap(tokens, "seg", 1)
    here = [tokens, swap(tokens, "mp", 1), by_z, swap(by_z, "mp", 1)]
    tied, table = lax.optimization_barrier((tokens, table))
    there = [swap(piece, "grp", 1) for piece in [tied] + here[1:]]

    source = assemble(place, here + there, segs)

    def cut(weight, at_low, at_c):
        return lax.dynamic_slice(
            weight, (0, at_low * (2 * width) + at_c * width), (weight.shape[0], width)
        )

    def columns_of(weight):
        leaving = jnp.concatenate([cut(weight, low, 1 - c), cut(weight, 1 - low, 1 - c)])
        arrived = swap(leaving, "grp", 1)
        deep = weight.shape[0]
        own = jnp.concatenate([cut(weight, low, c), arrived[:deep]])
        other = jnp.concatenate([cut(weight, 1 - low, c), arrived[deep:]])
        return spread(own, other)

    x_near, x_far = columns_of(x_weight)
    y_near, y_far = columns_of(y_weight)

    half = 2 * width
    out_columns = out_weight.shape[1]
    out_near, out_far = spread(
        lax.dynamic_slice(out_weight, (low * half, 0), (half, out_columns)),
        lax.dynamic_slice(out_weight, ((1 - low) * half, 0), (half, out_columns)),
    )
    diagonal = turn == 0
    out_pieces = []
    for mine, theirs in zip(out_near, out_far):
        kept = jnp.where(diagonal, mine, theirs)
        passed = jnp.where(diagonal, theirs, mine)
        out_pieces.append((kept, swap(passed, "mp", 1)))

    (x_part,) = project(source, 0, x_near, last=False)
    (x_proj,) = project(source, 1, x_far, before=x_part)
    (y_part,) = project(source, 0, y_near, last=False)

    decay, drive, parts, total = run_gates(
        place, x_proj, table, decay_gate, input_gate, taps
    )
    totals = [total] + [swap(total, "seg", 2 * j) for j in range(1, highs)]
    totals = jnp.stack(totals)
    totals = [totals] + [swap(totals, "grp", 2 * i) for i in range(1, outer)]
    totals = jnp.stack(totals).reshape(outer * highs * 2, *total.shape[1:])
    state = run_states(
        place, decay, drive, parts, totals, table, decay_gate, input_gate, taps, outer, highs
    )

    (gated,) = project(source, 1, y_far, before=y_part, state=state)
    gated_y = swap(gated, "mp", 1)
    gated_near = [gated, swap(gated, "grp", 1)]
    gated_far = [gated_y, swap(gated_y, "grp", 1)]
    nears = []
    for b in range(0, segs, 2):
        nears.append(mix_near(place, gated_near, [out_pieces[b][0], out_pieces[b + 1][0]]))

    groups = [(b, b + 1) for b in range(0, segs - 2, 2)] + [(segs - 2,), (segs - 1,)]
    stays, arrivals = [], {}
    for group in groups:
        name = group[0]
        pieces = [out_pieces[b][1] for b in group]
        leave, stay = mix_far(place, gated_far, pieces, nears[name // 2], name % 2)
        stays.append(stay)
        partner = name if len(group) == 2 else name ^ 1
        arrivals[partner] = swap(leave, "seg", 1)

    own_blocks, other_blocks = [], []
    for group, stay in zip(groups, stays):
        arrived = arrivals[group[0]]

        def done(at_c):
            shape = (rows, stay.shape[1])
            kept = lax.dynamic_slice(stay, (at_c * rows, 0), shape)
            late = lax.dynamic_slice(arrived, (at_c * rows, 0), shape)
            return (kept + late.astype(jnp.float32)).astype(jnp.bfloat16)

        own_blocks.append(done(c))
        other_blocks.append(swap(done(1 - c), "grp", 1))
    return place_columns(place, groups, own_blocks, other_blocks, out_columns)


def solution(mesh):
    grps, segs, mps = mesh.shape["grp"], mesh.shape["seg"], mesh.shape["mp"]
    powers = segs >= 4 and segs & (segs - 1) == 0
    fits = grps == 2 * mps and mps == 2 and powers
    in_specs = (
        P(("grp", "seg"), "mp"),
        P(("grp", "seg"), "mp"),
        P(("grp", "seg"), "mp"),
        P("mp", ("grp", "seg")),
        P(None, "mp"),
        P("mp"),
        P("mp", None, None),
        P("mp"),
        P("mp", None, None),
        P("mp"),
        P("mp"),
        P("mp"),
    )
    out_specs = P(("grp", "seg"), "mp")

    def local(*arrays):
        return (folded if fits else general)(*arrays)

    return jax.shard_map(local, mesh=mesh, in_specs=in_specs, out_specs=out_specs, check_vma=False)
```

profile of v0, /device:TPU:0, one launch (start us, length us, event | category | flops | bytes accessed | tf_op | source)
XLA Modules:
  0.0 336.4 jit_solution(11132732549332961697)
XLA Ops:
  0.0 3.1 collective-permute-start.1
  3.1 2.6 constant_dynamic-slice_fusion.2
  8.6 1.5 collective-permute-start
  10.2 16.2 %collective-permute-done.1.refs_2_ = bf16[256,2048]{1,0:T(8,128)(2,1)S(1)} collective-permute-done((bf16[256,2048]{1,0:T(8,128)(2,1)}, bf16[256,2048]{1,0:T(8,128)(2,1)S(1)}, u32[]{:S(2)}, u32[]{:S(2)}) %collective-permute-start.1) | collective-permute-done | bytes 1048608 | tf_op jit(solution)/shard_map/ppermute | solution.py:122
  26.4 1.7 collective-permute-start.2
  29.4 1.6 collective-permute-start.17
  32.0 2.7 collective-permute-start.19
  35.0 18.9 %collective-permute-done.17.refs_1_ = bf16[512,512]{1,0:T(8,128)(2,1)} collective-permute-done((bf16[512,512]{1,0:T(8,128)(2,1)S(1)}, bf16[512,512]{1,0:T(8,128)(2,1)}, u32[]{:S(2)}, u32[]{:S(2)}) %collective-permute-start.17) | collective-permute-done | bytes 524320 | tf_op jit(solution)/shard_map/ppermute | solution.py:122
  53.9 2.3 collective-permute-done.2.refs_3_
  56.3 14.1 %collective-permute-done.19.refs_2_ = bf16[512,512]{1,0:T(8,128)(2,1)} collective-permute-done((bf16[512,512]{1,0:T(8,128)(2,1)S(1)}, bf16[512,512]{1,0:T(8,128)(2,1)}, u32[]{:S(2)}, u32[]{:S(2)}) %collective-permute-start.19) | collective-permute-done | bytes 524320 | tf_op jit(solution)/shard_map/ppermute | solution.py:122
  71.9 10.6 %collective-permute-start.11 = (bf16[512,512]{1,0:T(8,128)(2,1)S(1)}, bf16[512,512]{1,0:T(8,128)(2,1)S(1)}, u32[]{:S(2)}, u32[]{:S(2)}) collective-permute-start(bf16[512,512]{1,0:T(8,128)(2,1)S(1)} %pad_maximum_fusion.1.refs_0_), channel_id=1, source_target_pairs={{0,4},{2,6},{4,0},{6,2},{1,5},{3,7},{5,1},{7,3},{8,12},{10,14},{12... | collective-permute-start | bytes 1572872 | tf_op jit(solution)/shard_map/ppermute | solution.py:122
  83.3 2.0 collective-permute-start.13
  85.3 32.2 %collective-permute-done.11.refs_2_ = bf16[512,512]{1,0:T(8,128)(2,1)S(1)} collective-permute-done((bf16[512,512]{1,0:T(8,128)(2,1)S(1)}, bf16[512,512]{1,0:T(8,128)(2,1)S(1)}, u32[]{:S(2)}, u32[]{:S(2)}) %collective-permute-start.11) | collective-permute-done | bytes 524320 | tf_op jit(solution)/shard_map/ppermute | solution.py:122
  117.5 1.6 collective-permute-start.18
  122.9 8.2 %set_together.1.source_ref = bf16[1024,4096]{1,0:T(8,128)(2,1)} custom-call(s32[7]{0:T(128)} %stack.89.place_ref, bf16[256,2048]{1,0:T(8,128)(2,1)} %refs_0_.1, bf16[256,2048]{1,0:T(8,128)(2,1)} %copy-done.9, bf16[256,2048]{1,0:T(8,128)(2,1)} %copy-done.7, bf16[256,2048]{1,0:T(8,128)(2,1)} %copy-done.10, bf16[256,2048]{1,0:T(8,128)(2,1)} %copy-done.8, ...), custom_call_target="tpu_custom_call" | custom-call | bytes 16777216 | tf_op jit(solution)/shard_map/set_together/pallas_call | solution.py:151
  131.1 6.5 %project.5.refs_4_ = f32[1024,512]{1,0:T(8,128)} custom-call(bf16[1024,4096]{1,0:T(8,128)(2,1)} %set_together.1.source_ref, bf16[512,512]{1,0:T(8,128)(2,1)} %copy-done.5, bf16[512,512]{1,0:T(8,128)(2,1)} %collective-permute-done.17.refs_1_, bf16[512,512]{1,0:T(8,128)(2,1)} %collective-permute-done.19.refs_2_, bf16[512,512]{1,0:T(8,128)(2,1)} %collective-permute-done.21.refs_3_), custom_call_target="tpu_custom_call" | custom-call | flops 2147483648 | bytes 6291456 | tf_op jit(solution)/shard_map/project/pallas_call | solution.py:228
  140.6 3.2 collective-permute-done.20.refs_2_
  145.3 9.8 %collective-permute-done.22.refs_3_ = bf16[512,512]{1,0:T(8,128)(2,1)} collective-permute-done((bf16[512,512]{1,0:T(8,128)(2,1)}, bf16[512,512]{1,0:T(8,128)(2,1)}, u32[]{:S(2)}, u32[]{:S(2)}) %collective-permute-start.22) | collective-permute-done | bytes 524320 | tf_op jit(solution)/shard_map/ppermute | solution.py:122
  155.2 6.5 %project.6.x_ref = bf16[1024,512]{1,0:T(8,128)(2,1)} custom-call(bf16[1024,4096]{1,0:T(8,128)(2,1)} %set_together.1.source_ref, bf16[512,512]{1,0:T(8,128)(2,1)} %copy-done.26, bf16[512,512]{1,0:T(8,128)(2,1)} %copy-done.27, bf16[512,512]{1,0:T(8,128)(2,1)} %copy-done.28, bf16[512,512]{1,0:T(8,128)(2,1)} %collective-permute-done.22.refs_3_, ...), custom_call_target="tpu_custom_call" | custom-call | flops 2147483648 | bytes 6291456 | tf_op jit(solution)/shard_map/project/pallas_call | solution.py:228
  161.7 11.1 %gates.1 = (f32[4,1024,128]{2,1,0:T(8,128)}, f32[4,1024,128]{2,1,0:T(8,128)}, f32[2,24,512]{2,1,0:T(8,128)}, f32[2,16,512]{2,1,0:T(8,128)}) custom-call(s32[7]{0:T(128)} %stack.89.place_ref, bf16[1024,512]{1,0:T(8,128)(2,1)} %project.6.x_ref, f32[16,2048]{1,0:T(8,128)} %stack.102.table_ref, bf16[8,256,256]{2,1,0:T(8,128)(2,1)} %decay_w.3, ...), custom_call_target="tpu_custom_call" | custom-call | flops 536870912 | bytes 5242880 | tf_op jit(solution)/shard_map/gates/pallas_call | solution.py:361
  172.8 2.1 collective-permute-start.23
  174.9 3.3 collective-permute-done.23
  179.0 1.6 collective-permute-start.24
  180.6 6.3 %project.4.refs_4_ = f32[1024,512]{1,0:T(8,128)} custom-call(bf16[1024,4096]{1,0:T(8,128)(2,1)} %set_together.1.source_ref, bf16[512,512]{1,0:T(8,128)(2,1)} %copy-done.4, bf16[512,512]{1,0:T(8,128)(2,1)} %collective-permute-done.9.refs_1_, bf16[512,512]{1,0:T(8,128)(2,1)} %copy-done.16, bf16[512,512]{1,0:T(8,128)(2,1)} %collective-permute-done.13.refs_3_), custom_call_target="tpu_custom_call" | custom-call | flops 2147483648 | bytes 6291456 | tf_op jit(solution)/shard_map/project/pallas_call | solution.py:228
  186.9 12.8 %collective-permute-done.24 = f32[2,2,16,512]{3,2,1,0:T(8,128)S(1)} collective-permute-done((f32[2,2,16,512]{3,2,1,0:T(8,128)S(1)}, f32[2,2,16,512]{3,2,1,0:T(8,128)S(1)}, u32[]{:S(2)}, u32[]{:S(2)}) %collective-permute-start.24) | collective-permute-done | bytes 131104 | tf_op jit(solution)/shard_map/ppermute | solution.py:122
  200.4 8.4 %states.1.refs_5_ = f32[4,1024,128]{2,1,0:T(8,128)} custom-call(s32[7]{0:T(128)} %stack.89.place_ref, f32[4,1024,128]{2,1,0:T(8,128)} %get-tuple-element.19.decay_ref, f32[4,1024,128]{2,1,0:T(8,128)} %get-tuple-element.20.drive_ref, f32[2,24,512]{2,1,0:T(8,128)} %get-tuple-element.21.part_ref, f32[8,16,512]{2,1,0:T(8,128)} %bitcast.25, ...), custom_call_target="tpu_custom_call" | custom-call | flops 5242880 | bytes 6291456 | tf_op jit(solution)/shard_map/states/pallas_call | solution.py:520
  210.7 7.2 %project.7.refs_0_ = bf16[1024,512]{1,0:T(8,128)(2,1)} custom-call(bf16[1024,4096]{1,0:T(8,128)(2,1)} %set_together.1.source_ref, bf16[512,512]{1,0:T(8,128)(2,1)} %copy-done.18, bf16[512,512]{1,0:T(8,128)(2,1)} %copy-done.19, bf16[512,512]{1,0:T(8,128)(2,1)} %copy-done.20, bf16[512,512]{1,0:T(8,128)(2,1)} %copy-done.21, f32[1024,512]{1,0:T(8,128)} %project.4.refs_4_, ...), custom_call_target="tpu_custom_call" | custom-call | flops 2147483648 | bytes 6291456 | tf_op jit(solution)/shard_map/project/pallas_call | solution.py:228
  218.4 2.1 constant_dynamic-slice_fusion
  220.5 1.7 collective-permute-start.29
  225.5 15.6 %collective-permute-done.29 = bf16[1024,256]{1,0:T(8,128)(2,1)} collective-permute-done((bf16[1024,256]{1,0:T(8,128)(2,1)}, bf16[1024,256]{1,0:T(8,128)(2,1)}, u32[]{:S(2)}, u32[]{:S(2)}) %collective-permute-start.29) | collective-permute-done | bytes 524320 | tf_op jit(solution)/shard_map/ppermute | solution.py:122
  241.1 1.5 collective-permute-start.30
  242.6 5.2 %collective-permute-done.37 = bf16[1024,256]{1,0:T(8,128)(2,1)} collective-permute-done((bf16[1024,256]{1,0:T(8,128)(2,1)}, bf16[1024,256]{1,0:T(8,128)(2,1)}, u32[]{:S(2)}, u32[]{:S(2)}) %collective-permute-start.37) | collective-permute-done | bytes 524320 | tf_op jit(solution)/shard_map/ppermute | solution.py:122
  249.8 1.9 broadcast_select_fusion.5
  251.8 14.4 %collective-permute-done.34 = bf16[1024,256]{1,0:T(8,128)(2,1)S(1)} collective-permute-done((bf16[1024,256]{1,0:T(8,128)(2,1)S(1)}, bf16[1024,256]{1,0:T(8,128)(2,1)S(1)}, u32[]{:S(2)}, u32[]{:S(2)}) %collective-permute-start.34) | collective-permute-done | bytes 524320 | tf_op jit(solution)/shard_map/ppermute | solution.py:122
  267.6 1.5 collective-permute-start.35
  269.1 2.1 broadcast_select_fusion.4
  271.8 2.0 broadcast_select_fusion
  273.8 3.0 collective-permute-done.35
  279.7 4.9 %mix_near.2.refs_4_ = f32[1024,512]{1,0:T(8,128)} custom-call(s32[7]{0:T(128)} %stack.89.place_ref, bf16[1024,512]{1,0:T(8,128)(2,1)} %project.7.refs_0_, bf16[1024,512]{1,0:T(8,128)(2,1)} %copy-done.3, bf16[1024,256]{1,0:T(8,128)(2,1)} %get-tuple-element.37.refs_2_, bf16[1024,256]{1,0:T(8,128)(2,1)} %get-tuple-element.35.refs_3_), custom_call_target="tpu_custom_call" | custom-call | flops 1073741824 | bytes 4194304 | tf_op jit(solution)/shard_map/mix_near/pallas_call | solution.py:560
  284.6 7.7 %collective-permute-done.31.refs_3_ = bf16[1024,256]{1,0:T(8,128)(2,1)} collective-permute-done((bf16[1024,256]{1,0:T(8,128)(2,1)S(1)}, bf16[1024,256]{1,0:T(8,128)(2,1)}, u32[]{:S(2)}, u32[]{:S(2)}) %collective-permute-start.31) | collective-permute-done | bytes 524320 | tf_op jit(solution)/shard_map/ppermute | solution.py:122
  293.3 6.3 %mix_far.3 = (bf16[512,512]{1,0:T(8,128)(2,1)}, f32[512,512]{1,0:T(8,128)}) custom-call(s32[7]{0:T(128)} %stack.89.place_ref, bf16[1024,512]{1,0:T(8,128)(2,1)} %copy-done, bf16[1024,512]{1,0:T(8,128)(2,1)} %copy-done.1, bf16[1024,256]{1,0:T(8,128)(2,1)} %collective-permute-done.28.refs_2_, bf16[1024,256]{1,0:T(8,128)(2,1)} %collective-permute-done.31.refs_3_, ...), custom_call_target="tpu_custom_call" | custom-call | flops 1073741824 | bytes 5767168 | tf_op jit(solution)/shard_map/mix_far/pallas_call | solution.py:613
  299.6 4.9 %mix_near.3.refs_3_ = f32[1024,512]{1,0:T(8,128)} custom-call(s32[7]{0:T(128)} %stack.89.place_ref, bf16[1024,512]{1,0:T(8,128)(2,1)} %project.7.refs_0_, bf16[1024,512]{1,0:T(8,128)(2,1)} %copy-done.3, bf16[1024,256]{1,0:T(8,128)(2,1)} %get-tuple-element.33.refs_2_, bf16[1024,256]{1,0:T(8,128)(2,1)} %get-tuple-element.32.refs_3_), custom_call_target="tpu_custom_call" | custom-call | flops 1073741824 | bytes 4194304 | tf_op jit(solution)/shard_map/mix_near/pallas_call | solution.py:560
  304.6 4.8 %collective-permute-done.36.refs_2_ = bf16[1024,256]{1,0:T(8,128)(2,1)S(1)} collective-permute-done((bf16[1024,256]{1,0:T(8,128)(2,1)S(1)}, bf16[1024,256]{1,0:T(8,128)(2,1)S(1)}, u32[]{:S(2)}, u32[]{:S(2)}) %collective-permute-start.36) | collective-permute-done | bytes 524320 | tf_op jit(solution)/shard_map/ppermute | solution.py:122
  310.1 5.2 %mix_far.4 = (bf16[512,256]{1,0:T(8,128)(2,1)}, f32[512,256]{1,0:T(8,128)}) custom-call(s32[7]{0:T(128)} %stack.89.place_ref, bf16[1024,512]{1,0:T(8,128)(2,1)} %copy-done, bf16[1024,512]{1,0:T(8,128)(2,1)} %copy-done.1, bf16[1024,256]{1,0:T(8,128)(2,1)} %copy-done.23, f32[1024,512]{1,0:T(8,128)} %mix_near.3.refs_3_), custom_call_target="tpu_custom_call" | custom-call | flops 536870912 | bytes 3932160 | tf_op jit(solution)/shard_map/mix_far/pallas_call | solution.py:613
  315.3 2.7 collective-permute-start.41
  318.8 5.2 %mix_far.5 = (bf16[512,256]{1,0:T(8,128)(2,1)}, f32[512,256]{1,0:T(8,128)}) custom-call(s32[7]{0:T(128)} %stack.89.place_ref, bf16[1024,512]{1,0:T(8,128)(2,1)} %copy-done, bf16[1024,512]{1,0:T(8,128)(2,1)} %copy-done.1, bf16[1024,256]{1,0:T(8,128)(2,1)} %copy-done.22, f32[1024,512]{1,0:T(8,128)} %mix_near.3.refs_3_), custom_call_target="tpu_custom_call" | custom-call | flops 536870912 | bytes 3932160 | tf_op jit(solution)/shard_map/mix_far/pallas_call | solution.py:613
  326.2 5.0 %collective-permute-done.40 = bf16[512,256]{1,0:T(8,128)(2,1)S(1)} collective-permute-done((bf16[512,256]{1,0:T(8,128)(2,1)}, bf16[512,256]{1,0:T(8,128)(2,1)S(1)}, u32[]{:S(2)}, u32[]{:S(2)}) %collective-permute-start.40) | collective-permute-done | bytes 262176 | tf_op jit(solution)/shard_map/ppermute | solution.py:122
  334.0 2.3 place.1
  (154 shorter events, 37.9 us)
Async XLA Ops:
  0.0 26.4 %collective-permute-start.1 = (bf16[256,2048]{1,0:T(8,128)(2,1)}, bf16[256,2048]{1,0:T(8,128)(2,1)S(1)}, u32[]{:S(2)}, u32[]{:S(2)}) collective-permute-start(bf16[256,2048]{1,0:T(8,128)(2,1)} %refs_0_.1), channel_id=1, source_target_pairs={{0,2},{2,0},{4,6},{6,4},{1,3},{3,1},{5,7},{7,5},{8,10},{10,8},{12,... | collective-permute-start | bytes 3145736 | tf_op jit(solution)/shard_map/ppermute | solution.py:122
  6.5 21.7 %collective-permute-start.15 = (bf16[512,512]{1,0:T(8,128)(2,1)}, bf16[512,512]{1,0:T(8,128)(2,1)}, u32[]{:S(2)}, u32[]{:S(2)}) collective-permute-start(bf16[512,512]{1,0:T(8,128)(2,1)} %pad_maximum_fusion.3), channel_id=1, source_target_pairs={{0,8},{8,0},{16,24},{24,16},{1,9},{9,1},{17,25},{25,17},{2,10},{10... | collective-permute-start | bytes 1572872 | tf_op jit(solution)/shard_map/ppermute | solution.py:122
  8.1 26.5 %collective-permute-start.3 = (bf16[256,2048]{1,0:T(8,128)(2,1)S(1)}, bf16[256,2048]{1,0:T(8,128)(2,1)S(1)}, u32[]{:S(2)}, u32[]{:S(2)}) collective-permute-start(bf16[256,2048]{1,0:T(8,128)(2,1)S(1)} %copy-done.6), channel_id=1, source_target_pairs={{0,8},{8,0},{16,24},{24,16},{1,9},{9,1},{17,25},{25,17},{2,10},{10... | collective-permute-start | bytes 3145736 | tf_op jit(solution)/shard_map/ppermute | solution.py:122
  8.6 26.2 %collective-permute-start = (bf16[256,2048]{1,0:T(8,128)(2,1)S(1)}, bf16[256,2048]{1,0:T(8,128)(2,1)S(1)}, u32[]{:S(2)}, u32[]{:S(2)}) collective-permute-start(bf16[256,2048]{1,0:T(8,128)(2,1)S(1)} %copy-done.6), channel_id=1, source_target_pairs={{0,1},{1,0},{2,3},{3,2},{4,5},{5,4},{6,7},{7,6},{8,9},{9,8},{10,11... | collective-permute-start | bytes 3145736 | tf_op jit(solution)/shard_map/ppermute | solution.py:122
  26.4 29.8 %collective-permute-start.2 = (bf16[256,2048]{1,0:T(8,128)(2,1)S(1)}, bf16[256,2048]{1,0:T(8,128)(2,1)S(1)}, u32[]{:S(2)}, u32[]{:S(2)}) collective-permute-start(bf16[256,2048]{1,0:T(8,128)(2,1)S(1)} %collective-permute-done.1.refs_2_), channel_id=1, source_target_pairs={{0,1},{1,0},{2,3},{3,2},{4,5},{5,4},{6,7},{7,6},{8,9},{9,8},{10,11... | collective-permute-start | bytes 3145736 | tf_op jit(solution)/shard_map/ppermute | solution.py:122
  28.2 3.8 %collective-permute-start.7 = (bf16[512,512]{1,0:T(8,128)(2,1)S(1)}, bf16[512,512]{1,0:T(8,128)(2,1)S(1)}, u32[]{:S(2)}, u32[]{:S(2)}) collective-permute-start(bf16[512,512]{1,0:T(8,128)(2,1)S(1)} %pad_maximum_fusion), channel_id=1, source_target_pairs={{0,8},{8,0},{16,24},{24,16},{1,9},{9,1},{17,25},{25,17},{2,10},{10... | collective-permute-start | bytes 1572872 | tf_op jit(solution)/shard_map/ppermute | solution.py:122
  29.4 24.5 %collective-permute-start.17 = (bf16[512,512]{1,0:T(8,128)(2,1)S(1)}, bf16[512,512]{1,0:T(8,128)(2,1)}, u32[]{:S(2)}, u32[]{:S(2)}) collective-permute-start(bf16[512,512]{1,0:T(8,128)(2,1)S(1)} %pad_maximum_fusion.5), channel_id=1, source_target_pairs={{0,2},{2,0},{4,6},{6,4},{1,3},{3,1},{5,7},{7,5},{8,10},{10,8},{12,... | collective-permute-start | bytes 1572872 | tf_op jit(solution)/shard_map/ppermute | solution.py:122
  32.0 99.1 %copy-start.5 = (bf16[512,512]{1,0:T(8,128)(2,1)}, bf16[512,512]{1,0:T(8,128)(2,1)S(1)}, u32[]{:S(2)}) copy-start(bf16[512,512]{1,0:T(8,128)(2,1)S(1)} %pad_maximum_fusion.4.refs_0_) | copy-start | bytes 1572868
  32.0 38.4 %collective-permute-start.19 = (bf16[512,512]{1,0:T(8,128)(2,1)S(1)}, bf16[512,512]{1,0:T(8,128)(2,1)}, u32[]{:S(2)}, u32[]{:S(2)}) collective-permute-start(bf16[512,512]{1,0:T(8,128)(2,1)S(1)} %pad_maximum_fusion.4.refs_0_), channel_id=1, source_target_pairs={{0,4},{2,6},{4,0},{6,2},{1,5},{3,7},{5,1},{7,3},{8,12},{10,14},{12... | collective-permute-start | bytes 1572872 | tf_op jit(solution)/shard_map/ppermute | solution.py:122
  34.7 82.9 %copy-start.8 = (bf16[256,2048]{1,0:T(8,128)(2,1)}, bf16[256,2048]{1,0:T(8,128)(2,1)S(1)}, u32[]{:S(2)}) copy-start(bf16[256,2048]{1,0:T(8,128)(2,1)S(1)} %collective-permute-done.3.refs_4_) | copy-start | bytes 3145732
  34.7 37.2 %collective-permute-start.21 = (bf16[512,512]{1,0:T(8,128)(2,1)S(1)}, bf16[512,512]{1,0:T(8,128)(2,1)}, u32[]{:S(2)}, u32[]{:S(2)}) collective-permute-start(bf16[512,512]{1,0:T(8,128)(2,1)S(1)} %pad_maximum_fusion.5), channel_id=1, source_target_pairs={{0,6},{2,4},{4,2},{6,0},{1,7},{3,5},{5,3},{7,1},{8,14},{10,12},{12... | collective-permute-start | bytes 1572872 | tf_op jit(solution)/shard_map/ppermute | solution.py:122
  34.9 84.2 %copy-start.9 = (bf16[256,2048]{1,0:T(8,128)(2,1)}, bf16[256,2048]{1,0:T(8,128)(2,1)S(1)}, u32[]{:S(2)}) copy-start(bf16[256,2048]{1,0:T(8,128)(2,1)S(1)} %collective-permute-done.refs_1_) | copy-start | bytes 3145732
  34.9 82.6 %collective-permute-start.5 = (bf16[256,2048]{1,0:T(8,128)(2,1)S(1)}, bf16[256,2048]{1,0:T(8,128)(2,1)S(1)}, u32[]{:S(2)}, u32[]{:S(2)}) collective-permute-start(bf16[256,2048]{1,0:T(8,128)(2,1)S(1)} %collective-permute-done.1.refs_2_), channel_id=1, source_target_pairs={{0,8},{8,0},{16,24},{24,16},{1,9},{9,1},{17,25},{25,17},{2,10},{10... | collective-permute-start | bytes 3145736 | tf_op jit(solution)/shard_map/ppermute | solution.py:122
  53.9 65.2 %collective-permute-start.4 = (bf16[256,2048]{1,0:T(8,128)(2,1)S(1)}, bf16[256,2048]{1,0:T(8,128)(2,1)S(1)}, u32[]{:S(2)}, u32[]{:S(2)}) collective-permute-start(bf16[256,2048]{1,0:T(8,128)(2,1)S(1)} %collective-permute-done.refs_1_), channel_id=1, source_target_pairs={{0,8},{8,0},{16,24},{24,16},{1,9},{9,1},{17,25},{25,17},{2,10},{10... | collective-permute-start | bytes 3145736 | tf_op jit(solution)/shard_map/ppermute | solution.py:122
  56.2 63.5 %collective-permute-start.6 = (bf16[256,2048]{1,0:T(8,128)(2,1)S(1)}, bf16[256,2048]{1,0:T(8,128)(2,1)S(1)}, u32[]{:S(2)}, u32[]{:S(2)}) collective-permute-start(bf16[256,2048]{1,0:T(8,128)(2,1)S(1)} %collective-permute-done.2.refs_3_), channel_id=1, source_target_pairs={{0,8},{8,0},{16,24},{24,16},{1,9},{9,1},{17,25},{25,17},{2,10},{10... | collective-permute-start | bytes 3145736 | tf_op jit(solution)/shard_map/ppermute | solution.py:122
  70.4 12.9 %collective-permute-start.16 = (bf16[512,512]{1,0:T(8,128)(2,1)S(1)}, bf16[512,512]{1,0:T(8,128)(2,1)S(1)}, u32[]{:S(2)}, u32[]{:S(2)}) collective-permute-start(bf16[512,512]{1,0:T(8,128)(2,1)S(1)} %pad_maximum_fusion.4.refs_0_), channel_id=1, source_target_pairs={{0,16},{8,24},{16,0},{24,8},{1,17},{9,25},{17,1},{25,9},{2,18},{10... | collective-permute-start | bytes 1572872 | tf_op jit(solution)/shard_map/ppermute | solution.py:122
  71.9 45.6 %collective-permute-start.11 = (bf16[512,512]{1,0:T(8,128)(2,1)S(1)}, bf16[512,512]{1,0:T(8,128)(2,1)S(1)}, u32[]{:S(2)}, u32[]{:S(2)}) collective-permute-start(bf16[512,512]{1,0:T(8,128)(2,1)S(1)} %pad_maximum_fusion.1.refs_0_), channel_id=1, source_target_pairs={{0,4},{2,6},{4,0},{6,2},{1,5},{3,7},{5,1},{7,3},{8,12},{10,14},{12... | collective-permute-start | bytes 1572872 | tf_op jit(solution)/shard_map/ppermute | solution.py:122
  83.3 54.3 %collective-permute-start.13 = (bf16[512,512]{1,0:T(8,128)(2,1)}, bf16[512,512]{1,0:T(8,128)(2,1)}, u32[]{:S(2)}, u32[]{:S(2)}) collective-permute-start(bf16[512,512]{1,0:T(8,128)(2,1)} %pad_maximum_fusion.2), channel_id=1, source_target_pairs={{0,6},{2,4},{4,2},{6,0},{1,7},{3,5},{5,3},{7,1},{8,14},{10,12},{12... | collective-permute-start | bytes 1572872 | tf_op jit(solution)/shard_map/ppermute | solution.py:122
  117.5 21.0 %collective-permute-start.9 = (bf16[512,512]{1,0:T(8,128)(2,1)}, bf16[512,512]{1,0:T(8,128)(2,1)}, u32[]{:S(2)}, u32[]{:S(2)}) collective-permute-start(bf16[512,512]{1,0:T(8,128)(2,1)} %pad_maximum_fusion.2), channel_id=1, source_target_pairs={{0,2},{2,0},{4,6},{6,4},{1,3},{3,1},{5,7},{7,5},{8,10},{10,8},{12,... | collective-permute-start | bytes 1572872 | tf_op jit(solution)/shard_map/ppermute | solution.py:122
  117.5 22.1 %collective-permute-start.18 = (bf16[512,512]{1,0:T(8,128)(2,1)}, bf16[512,512]{1,0:T(8,128)(2,1)S(1)}, u32[]{:S(2)}, u32[]{:S(2)}) collective-permute-start(bf16[512,512]{1,0:T(8,128)(2,1)} %collective-permute-done.17.refs_1_), channel_id=1, source_target_pairs={{0,16},{8,24},{16,0},{24,8},{1,17},{9,25},{17,1},{25,9},{2,18},{10... | collective-permute-start | bytes 1572872 | tf_op jit(solution)/shard_map/ppermute | solution.py:122
  119.1 24.7 %collective-permute-start.20 = (bf16[512,512]{1,0:T(8,128)(2,1)}, bf16[512,512]{1,0:T(8,128)(2,1)S(1)}, u32[]{:S(2)}, u32[]{:S(2)}) collective-permute-start(bf16[512,512]{1,0:T(8,128)(2,1)} %collective-permute-done.19.refs_2_), channel_id=1, source_target_pairs={{0,16},{8,24},{16,0},{24,8},{1,17},{9,25},{17,1},{25,9},{2,18},{10... | collective-permute-start | bytes 1572872 | tf_op jit(solution)/shard_map/ppermute | solution.py:122
  121.1 34.1 %collective-permute-start.22 = (bf16[512,512]{1,0:T(8,128)(2,1)}, bf16[512,512]{1,0:T(8,128)(2,1)}, u32[]{:S(2)}, u32[]{:S(2)}) collective-permute-start(bf16[512,512]{1,0:T(8,128)(2,1)} %collective-permute-done.21.refs_3_), channel_id=1, source_target_pairs={{0,16},{8,24},{16,0},{24,8},{1,17},{9,25},{17,1},{25,9},{2,18},{10... | collective-permute-start | bytes 1572872 | tf_op jit(solution)/shard_map/ppermute | solution.py:122
  137.6 71.2 %collective-permute-start.8 = (bf16[512,512]{1,0:T(8,128)(2,1)S(1)}, bf16[512,512]{1,0:T(8,128)(2,1)S(1)}, u32[]{:S(2)}, u32[]{:S(2)}) collective-permute-start(bf16[512,512]{1,0:T(8,128)(2,1)S(1)} %pad_maximum_fusion.1.refs_0_), channel_id=1, source_target_pairs={{0,16},{8,24},{16,0},{24,8},{1,17},{9,25},{17,1},{25,9},{2,18},{10... | collective-permute-start | bytes 1572872 | tf_op jit(solution)/shard_map/ppermute | solution.py:122
  138.5 70.2 %collective-permute-start.10 = (bf16[512,512]{1,0:T(8,128)(2,1)}, bf16[512,512]{1,0:T(8,128)(2,1)S(1)}, u32[]{:S(2)}, u32[]{:S(2)}) collective-permute-start(bf16[512,512]{1,0:T(8,128)(2,1)} %collective-permute-done.9.refs_1_), channel_id=1, source_target_pairs={{0,16},{8,24},{16,0},{24,8},{1,17},{9,25},{17,1},{25,9},{2,18},{10... | collective-permute-start | bytes 1572872 | tf_op jit(solution)/shard_map/ppermute | solution.py:122
  139.7 69.1 %collective-permute-start.12 = (bf16[512,512]{1,0:T(8,128)(2,1)S(1)}, bf16[512,512]{1,0:T(8,128)(2,1)S(1)}, u32[]{:S(2)}, u32[]{:S(2)}) collective-permute-start(bf16[512,512]{1,0:T(8,128)(2,1)S(1)} %copy-done.17), channel_id=1, source_target_pairs={{0,16},{8,24},{16,0},{24,8},{1,17},{9,25},{17,1},{25,9},{2,18},{10... | collective-permute-start | bytes 1572872 | tf_op jit(solution)/shard_map/ppermute | solution.py:122
  143.9 65.0 %collective-permute-start.14 = (bf16[512,512]{1,0:T(8,128)(2,1)}, bf16[512,512]{1,0:T(8,128)(2,1)S(1)}, u32[]{:S(2)}, u32[]{:S(2)}) collective-permute-start(bf16[512,512]{1,0:T(8,128)(2,1)} %collective-permute-done.13.refs_3_), channel_id=1, source_target_pairs={{0,16},{8,24},{16,0},{24,8},{1,17},{9,25},{17,1},{25,9},{2,18},{10... | collective-permute-start | bytes 1572872 | tf_op jit(solution)/shard_map/ppermute | solution.py:122
  172.8 5.4 %collective-permute-start.23 = (f32[2,16,512]{2,1,0:T(8,128)}, f32[2,16,512]{2,1,0:T(8,128)S(1)}, u32[]{:S(2)}, u32[]{:S(2)}) collective-permute-start(f32[2,16,512]{2,1,0:T(8,128)} %get-tuple-element.22), channel_id=1, source_target_pairs={{0,4},{2,6},{4,0},{6,2},{1,5},{3,7},{5,1},{7,3},{8,12},{10,14},{12... | collective-permute-start | bytes 196616 | tf_op jit(solution)/shard_map/ppermute | solution.py:122
  179.0 20.6 %collective-permute-start.24 = (f32[2,2,16,512]{3,2,1,0:T(8,128)S(1)}, f32[2,2,16,512]{3,2,1,0:T(8,128)S(1)}, u32[]{:S(2)}, u32[]{:S(2)}) collective-permute-start(f32[2,2,16,512]{3,2,1,0:T(8,128)S(1)} %get-tuple-element.58), channel_id=1, source_target_pairs={{0,16},{8,24},{16,0},{24,8},{1,17},{9,25},{17,1},{25,9},{2,18},{10... | collective-permute-start | bytes 393224 | tf_op jit(solution)/shard_map/ppermute | solution.py:122
  217.9 31.4 %collective-permute-start.25 = (bf16[1024,512]{1,0:T(8,128)(2,1)}, bf16[1024,512]{1,0:T(8,128)(2,1)S(1)}, u32[]{:S(2)}, u32[]{:S(2)}) collective-permute-start(bf16[1024,512]{1,0:T(8,128)(2,1)} %project.7.refs_0_), channel_id=1, source_target_pairs={{0,1},{1,0},{2,3},{3,2},{4,5},{5,4},{6,7},{7,6},{8,9},{9,8},{10,11... | collective-permute-start | bytes 3145736 | tf_op jit(solution)/shard_map/ppermute | solution.py:122
  220.5 20.6 %collective-permute-start.29 = (bf16[1024,256]{1,0:T(8,128)(2,1)}, bf16[1024,256]{1,0:T(8,128)(2,1)}, u32[]{:S(2)}, u32[]{:S(2)}) collective-permute-start(bf16[1024,256]{1,0:T(8,128)(2,1)} %get-tuple-element.39), channel_id=1, source_target_pairs={{0,2},{2,0},{4,6},{6,4},{1,3},{3,1},{5,7},{7,5},{8,10},{10,8},{12,... | collective-permute-start | bytes 1572872 | tf_op jit(solution)/shard_map/ppermute | solution.py:122
  222.2 25.6 %collective-permute-start.37 = (bf16[1024,256]{1,0:T(8,128)(2,1)}, bf16[1024,256]{1,0:T(8,128)(2,1)}, u32[]{:S(2)}, u32[]{:S(2)}) collective-permute-start(bf16[1024,256]{1,0:T(8,128)(2,1)} %get-tuple-element.39), channel_id=1, source_target_pairs={{0,6},{2,4},{4,2},{6,0},{1,7},{3,5},{5,3},{7,1},{8,14},{10,12},{12... | collective-permute-start | bytes 1572872 | tf_op jit(solution)/shard_map/ppermute | solution.py:122
  223.4 25.9 %collective-permute-start.27 = (bf16[1024,256]{1,0:T(8,128)(2,1)S(1)}, bf16[1024,256]{1,0:T(8,128)(2,1)}, u32[]{:S(2)}, u32[]{:S(2)}) collective-permute-start(bf16[1024,256]{1,0:T(8,128)(2,1)S(1)} %get-tuple-element.40), channel_id=1, source_target_pairs={{0,16},{8,24},{16,0},{24,8},{1,17},{9,25},{17,1},{25,9},{2,18},{10... | collective-permute-start | bytes 1572872 | tf_op jit(solution)/shard_map/ppermute | solution.py:122
  224.9 41.3 %collective-permute-start.34 = (bf16[1024,256]{1,0:T(8,128)(2,1)S(1)}, bf16[1024,256]{1,0:T(8,128)(2,1)S(1)}, u32[]{:S(2)}, u32[]{:S(2)}) collective-permute-start(bf16[1024,256]{1,0:T(8,128)(2,1)S(1)} %get-tuple-element.40), channel_id=1, source_target_pairs={{0,4},{2,6},{4,0},{6,2},{1,5},{3,7},{5,1},{7,3},{8,12},{10,14},{12... | collective-permute-start | bytes 1572872 | tf_op jit(solution)/shard_map/ppermute | solution.py:122
  241.1 26.5 %collective-permute-start.30 = (bf16[1024,256]{1,0:T(8,128)(2,1)}, bf16[1024,256]{1,0:T(8,128)(2,1)}, u32[]{:S(2)}, u32[]{:S(2)}) collective-permute-start(bf16[1024,256]{1,0:T(8,128)(2,1)} %collective-permute-done.29), channel_id=1, source_target_pairs={{0,16},{8,24},{16,0},{24,8},{1,17},{9,25},{17,1},{25,9},{2,18},{10... | collective-permute-start | bytes 1572872 | tf_op jit(solution)/shard_map/ppermute | solution.py:122
  247.8 23.4 %collective-permute-start.38 = (bf16[1024,256]{1,0:T(8,128)(2,1)}, bf16[1024,256]{1,0:T(8,128)(2,1)S(1)}, u32[]{:S(2)}, u32[]{:S(2)}) collective-permute-start(bf16[1024,256]{1,0:T(8,128)(2,1)} %collective-permute-done.37), channel_id=1, source_target_pairs={{0,16},{8,24},{16,0},{24,8},{1,17},{9,25},{17,1},{25,9},{2,18},{10... | collective-permute-start | bytes 1572872 | tf_op jit(solution)/shard_map/ppermute | solution.py:122
  249.3 28.9 %collective-permute-start.32 = (bf16[1024,512]{1,0:T(8,128)(2,1)S(1)}, bf16[1024,512]{1,0:T(8,128)(2,1)S(1)}, u32[]{:S(2)}, u32[]{:S(2)}) collective-permute-start(bf16[1024,512]{1,0:T(8,128)(2,1)S(1)} %copy-done.2), channel_id=1, source_target_pairs={{0,8},{8,0},{16,24},{24,16},{1,9},{9,1},{17,25},{25,17},{2,10},{10... | collective-permute-start | bytes 3145736 | tf_op jit(solution)/shard_map/ppermute | solution.py:122
  249.3 43.0 %collective-permute-start.26 = (bf16[1024,512]{1,0:T(8,128)(2,1)S(1)}, bf16[1024,512]{1,0:T(8,128)(2,1)S(1)}, u32[]{:S(2)}, u32[]{:S(2)}) collective-permute-start(bf16[1024,512]{1,0:T(8,128)(2,1)S(1)} %collective-permute-done.25.refs_0_), channel_id=1, source_target_pairs={{0,8},{8,0},{16,24},{24,16},{1,9},{9,1},{17,25},{25,17},{2,10},{10... | collective-permute-start | bytes 3145736 | tf_op jit(solution)/shard_map/ppermute | solution.py:122
  266.2 18.4 %collective-permute-start.28 = (bf16[1024,256]{1,0:T(8,128)(2,1)S(1)}, bf16[1024,256]{1,0:T(8,128)(2,1)}, u32[]{:S(2)}, u32[]{:S(2)}) collective-permute-start(bf16[1024,256]{1,0:T(8,128)(2,1)S(1)} %get-tuple-element.38), channel_id=1, source_target_pairs={{0,1},{1,0},{2,3},{3,2},{4,5},{5,4},{6,7},{7,6},{8,9},{9,8},{10,11... | collective-permute-start | bytes 1572872 | tf_op jit(solution)/shard_map/ppermute | solution.py:122
  267.6 9.2 %collective-permute-start.35 = (bf16[1024,256]{1,0:T(8,128)(2,1)S(1)}, bf16[1024,256]{1,0:T(8,128)(2,1)S(1)}, u32[]{:S(2)}, u32[]{:S(2)}) collective-permute-start(bf16[1024,256]{1,0:T(8,128)(2,1)S(1)} %collective-permute-done.34), channel_id=1, source_target_pairs={{0,16},{8,24},{16,0},{24,8},{1,17},{9,25},{17,1},{25,9},{2,18},{10... | collective-permute-start | bytes 1572872 | tf_op jit(solution)/shard_map/ppermute | solution.py:122
  271.2 21.1 %collective-permute-start.31 = (bf16[1024,256]{1,0:T(8,128)(2,1)S(1)}, bf16[1024,256]{1,0:T(8,128)(2,1)}, u32[]{:S(2)}, u32[]{:S(2)}) collective-permute-start(bf16[1024,256]{1,0:T(8,128)(2,1)S(1)} %get-tuple-element.36), channel_id=1, source_target_pairs={{0,1},{1,0},{2,3},{3,2},{4,5},{5,4},{6,7},{7,6},{8,9},{9,8},{10,11... | collective-permute-start | bytes 1572872 | tf_op jit(solution)/shard_map/ppermute | solution.py:122
  276.8 41.2 %collective-permute-start.39 = (bf16[1024,256]{1,0:T(8,128)(2,1)S(1)}, bf16[1024,256]{1,0:T(8,128)(2,1)S(1)}, u32[]{:S(2)}, u32[]{:S(2)}) collective-permute-start(bf16[1024,256]{1,0:T(8,128)(2,1)S(1)} %get-tuple-element.31), channel_id=1, source_target_pairs={{0,1},{1,0},{2,3},{3,2},{4,5},{5,4},{6,7},{7,6},{8,9},{9,8},{10,11... | collective-permute-start | bytes 1572872 | tf_op jit(solution)/shard_map/ppermute | solution.py:122
  278.2 31.1 %collective-permute-start.36 = (bf16[1024,256]{1,0:T(8,128)(2,1)S(1)}, bf16[1024,256]{1,0:T(8,128)(2,1)S(1)}, u32[]{:S(2)}, u32[]{:S(2)}) collective-permute-start(bf16[1024,256]{1,0:T(8,128)(2,1)S(1)} %get-tuple-element.34), channel_id=1, source_target_pairs={{0,1},{1,0},{2,3},{3,2},{4,5},{5,4},{6,7},{7,6},{8,9},{9,8},{10,11... | collective-permute-start | bytes 1572872 | tf_op jit(solution)/shard_map/ppermute | solution.py:122
  299.6 24.4 %collective-permute-start.33 = (bf16[512,512]{1,0:T(8,128)(2,1)}, bf16[512,512]{1,0:T(8,128)(2,1)S(1)}, u32[]{:S(2)}, u32[]{:S(2)}) collective-permute-start(bf16[512,512]{1,0:T(8,128)(2,1)} %get-tuple-element.24), channel_id=1, source_target_pairs={{0,2},{2,0},{4,6},{6,4},{1,3},{3,1},{5,7},{7,5},{8,10},{10,8},{12,... | collective-permute-start | bytes 1572872 | tf_op jit(solution)/shard_map/ppermute | solution.py:122
  315.3 9.6 %collective-permute-start.41 = (bf16[512,256]{1,0:T(8,128)(2,1)}, bf16[512,256]{1,0:T(8,128)(2,1)S(1)}, u32[]{:S(2)}, u32[]{:S(2)}) collective-permute-start(bf16[512,256]{1,0:T(8,128)(2,1)} %get-tuple-element.28), channel_id=1, source_target_pairs={{0,2},{2,0},{4,6},{6,4},{1,3},{3,1},{5,7},{7,5},{8,10},{10,8},{12,... | collective-permute-start | bytes 786440 | tf_op jit(solution)/shard_map/ppermute | solution.py:122
  324.0 7.3 %collective-permute-start.40 = (bf16[512,256]{1,0:T(8,128)(2,1)}, bf16[512,256]{1,0:T(8,128)(2,1)S(1)}, u32[]{:S(2)}, u32[]{:S(2)}) collective-permute-start(bf16[512,256]{1,0:T(8,128)(2,1)} %get-tuple-element.26), channel_id=1, source_target_pairs={{0,2},{2,0},{4,6},{6,4},{1,3},{3,1},{5,7},{7,5},{8,10},{10,8},{12,... | collective-permute-start | bytes 786440 | tf_op jit(solution)/shard_map/ppermute | solution.py:122
  325.0 8.3 %collective-permute-start.42 = (bf16[256,512]{1,0:T(8,128)(2,1)S(1)}, bf16[256,512]{1,0:T(8,128)(2,1)S(1)}, u32[]{:S(2)}, u32[]{:S(2)}) collective-permute-start(bf16[256,512]{1,0:T(8,128)(2,1)S(1)} %get-tuple-element.29), channel_id=1, source_target_pairs={{0,8},{8,0},{16,24},{24,16},{1,9},{9,1},{17,25},{25,17},{2,10},{10... | collective-permute-start | bytes 786440 | tf_op jit(solution)/shard_map/ppermute | solution.py:122
  325.7 6.2 %collective-permute-start.44 = (bf16[256,256]{1,0:T(8,128)(2,1)S(1)}, bf16[256,256]{1,0:T(8,128)(2,1)S(1)}, u32[]{:S(2)}, u32[]{:S(2)}) collective-permute-start(bf16[256,256]{1,0:T(8,128)(2,1)S(1)} %get-tuple-element.49), channel_id=1, source_target_pairs={{0,8},{8,0},{16,24},{24,16},{1,9},{9,1},{17,25},{25,17},{2,10},{10... | collective-permute-start | bytes 393224 | tf_op jit(solution)/shard_map/ppermute | solution.py:122
  331.9 1.3 collective-permute-start.43
  (35 other events, 369.7 us)
where the time goes:
time: 337 us; the launch traced here: 336 us
  waiting for transfers between devices  170 us (50%)
  Pallas kernels  83 us (25%)
  starting transfers between devices  54.8 us (16%)
  local copies, waits for them, and re-layouts  14.5 us (4%)
  other arithmetic  13.6 us (4%)
    ppermute x45, waiting for transfers between devices, swap(): return lax.ppermute(value, axis, [(i, i ^ bit) for i in range(count)])  170 us
    ppermute x45, starting transfers between devices, swap(): return lax.ppermute(value, axis, [(i, i ^ bit) for i in range(count)])  54.8 us
    pallas_call x4, Pallas kernels, project(): pl.pallas_call(kernel, grid=(tokens_here // rows,), out_shape=out_shape,...  26.4 us
    pallas_call x3, Pallas kernels, mix_far(): pl.pallas_call(kernel, grid_spec=grid_spec, out_shape=[jax.ShapeDtypeStru...  16.7 us
    pallas_call x1, Pallas kernels, run_gates(): pl.pallas_call(kernel, grid_spec=grid_spec, out_shape=[jax.ShapeDtypeStru...  11.1 us
    pallas_call x2, Pallas kernels, mix_near(): pl.pallas_call(kernel, grid=(4,), out_shape=jax.ShapeDtypeStruct((tokens_...  9.83 us
    pallas_call x1, Pallas kernels, run_states(): pl.pallas_call(kernel, grid_spec=grid_spec, out_shape=jax.ShapeDtypeStruc...  8.38 us
    pallas_call x1, Pallas kernels, assemble(): pl.pallas_call(kernel, out_shape=jax.ShapeDtypeStruct((2 * lows * rows, 2...  8.2 us
  transfers between devices with their start and end apart: 45, of which 17 were waited for; matrix products, arithmetic and copies ran while one was open for 6% of the time, Pallas kernels for 22%

commit v1 on v0

--- a/solution.py
+++ b/solution.py
@@ -575,48 +575,59 @@
     )(place, *parts, *pieces)
 
 
-def mix_far(place, parts, pieces, near, column):
+def mix_far(place, parts, pieces, near):
     tokens_here, deep = parts[0].shape
     width = pieces[0].shape[1]
     rows = tokens_here // 4
     count = len(pieces)
+    parts = [value.reshape(2, 2, rows, deep) for value in parts]
+    near = near.reshape(2, 2, rows, count * width)
 
     def kernel(place_ref, *refs):
-        near_ref, leave_ref, stay_ref = refs[-3:]
-        blocks = products(place_ref[0], refs[:2], refs[2:-3])
-        blocks = [
-            block + near_ref[:, b * width : (b + 1) * width] for b, block in enumerate(blocks)
-        ]
-
-        @pl.when(pl.program_id(1) == 0)
+        near_ref, leaves, stays = refs[-5], refs[-4:-2], refs[-2:]
+        c = place_ref[0]
+        gated = [ref[...].reshape(2 * rows, deep) for ref in refs[:2]]
+        blocks = products(c, gated, refs[2:-5])
+        sums = near_ref[...].reshape(2 * rows, count * width)
+        blocks = [block + sums[:, b * width : (b + 1) * width] for b, block in enumerate(blocks)]
+
+        def write(targets, order):
+            for at_c in range(2):
+
+                @pl.when(c == at_c)
+                def write_runs():
+                    for e, target in enumerate(targets):
+                        run = at_c ^ e
+                        for b in range(count):
+                            at = order(b) * width
+                            target[:, at : at + width] = blocks[b][
+                                run * rows : (run + 1) * rows
+                            ].astype(target.dtype)
+
+        @pl.when(pl.program_id(0) == 0)
         def leave():
-            for b in range(count):
-                at = (count - 1 - b) * width
-                leave_ref[:, at : at + width] = blocks[b].astype(jnp.bfloat16)
-
-        @pl.when(pl.program_id(1) == 1)
+            write(leaves, lambda b: count - 1 - b)
+
+        @pl.when(pl.program_id(0) == 1)
         def stay():
-            for b in range(count):
-                stay_ref[:, b * width : (b + 1) * width] = blocks[b]
-
-    def row(r, f, p):
-        return r * 2 + (1 - f ^ p[6])
+            write(stays, lambda b: b)
+
+    def lows(f, p):
+        return (0, 1 - f ^ p[6], 0, 0)
 
     grid_spec = pltpu.PrefetchScalarGridSpec(
         num_scalar_prefetch=1,
-        grid=(2, 2),
-        in_specs=[pl.BlockSpec((rows, deep), lambda r, f, p: (row(r, f, p), 0)) for _ in parts]
-        + [pl.BlockSpec(piece.shape, lambda r, f, p: (0, 0)) for piece in pieces]
-        + [pl.BlockSpec((rows, count * width), lambda r, f, p: (row(r, f, p), column))],
-        out_specs=[pl.BlockSpec((rows, count * width), lambda r, f, p: (r, 0))] * 2,
-    )
+        grid=(2,),
+        in_specs=[pl.BlockSpec((2, 1, rows, deep), lows) for _ in parts]
+        + [pl.BlockSpec(piece.shape, lambda f, p: (0, 0)) for piece in pieces]
+        + [pl.BlockSpec((2, 1, rows, count * width), lows)],
+        out_specs=[pl.BlockSpec((rows, count * width), lambda f, p: (0, 0))] * 4,
+    )
+    kinds = [jnp.bfloat16, jnp.bfloat16, jnp.float32, jnp.bfloat16]
     return pl.pallas_call(
         kernel,
         grid_spec=grid_spec,
-        out_shape=[
-            jax.ShapeDtypeStruct((2 * rows, count * width), jnp.bfloat16),
-            jax.ShapeDtypeStruct((2 * rows, count * width), jnp.float32),
-        ],
+        out_shape=[jax.ShapeDtypeStruct((rows, count * width), kind) for kind in kinds],
         compiler_params=pltpu.CompilerParams(vmem_limit_bytes=GRANT),
         cost_estimate=pl.CostEstimate(
             flops=4 * count * tokens_here * deep * width,
@@ -627,8 +638,8 @@
     )(place, *parts, *pieces, near)
 
 
-def place_columns(place, groups, own, other, block):
-    rows = own[0].shape[0]
+def place_columns(place, groups, terms, block):
+    rows = terms[0].shape[0]
     segs = sum(len(group) for group in groups)
 
     def kernel(place_ref, *refs):
@@ -638,16 +649,19 @@
             for j, b in enumerate(group):
                 for d in range(2):
                     at = pl.multiple_of(((c ^ d) * segs + (z ^ b)) * block, block)
-                    from_ref = refs[d * len(groups) + i]
-                    whole[:, pl.ds(at, block)] = from_ref[:, j * block : (j + 1) * block]
+                    one, two = (
+                        ref[:, j * block : (j + 1) * block].astype(jnp.float32)
+                        for ref in refs[4 * i + 2 * d : 4 * i + 2 * d + 2]
+                    )
+                    whole[:, pl.ds(at, block)] = (one + two).astype(whole.dtype)
 
     return pl.pallas_call(
         kernel,
-        out_shape=jax.ShapeDtypeStruct((rows, 2 * segs * block), own[0].dtype),
-        in_specs=[SMEM] + [VMEM] * (2 * len(own)),
+        out_shape=jax.ShapeDtypeStruct((rows, 2 * segs * block), jnp.bfloat16),
+        in_specs=[SMEM] + [VMEM] * len(terms),
         out_specs=VMEM,
         name="place",
-    )(place, *own, *other)
+    )(place, *terms)
 
 
 def folded(
@@ -755,33 +769,28 @@
     gated_y = swap(gated, "mp", 1)
     gated_near = [gated, swap(gated, "grp", 1)]
     gated_far = [gated_y, swap(gated_y, "grp", 1)]
+    groups = [(b, b + 1) for b in range(0, segs - 2, 2)] + [(segs - 2,), (segs - 1,)]
     nears = []
-    for b in range(0, segs, 2):
-        nears.append(mix_near(place, gated_near, [out_pieces[b][0], out_pieces[b + 1][0]]))
-
-    groups = [(b, b + 1) for b in range(0, segs - 2, 2)] + [(segs - 2,), (segs - 1,)]
-    stays, arrivals = [], {}
     for group in groups:
+        nears.append(mix_near(place, gated_near, [out_pieces[b][0] for b in group]))
+
+    crossed = [
+        (og * segs + oz, (og ^ 1) * segs + (oz ^ 1)) for og in range(grps) for oz in range(segs)
+    ]
+    kept, arrived = [], {}
+    for group, near in zip(groups, nears):
         name = group[0]
         pieces = [out_pieces[b][1] for b in group]
-        leave, stay = mix_far(place, gated_far, pieces, nears[name // 2], name % 2)
-        stays.append(stay)
+        leave, leave_far, stay, stay_far = mix_far(place, gated_far, pieces, near)
+        kept.append((stay, swap(stay_far, "grp", 1)))
+        over = lax.ppermute(leave_far, ("grp", "seg"), crossed)
         partner = name if len(group) == 2 else name ^ 1
-        arrivals[partner] = swap(leave, "seg", 1)
-
-    own_blocks, other_blocks = [], []
-    for group, stay in zip(groups, stays):
-        arrived = arrivals[group[0]]
-
-        def done(at_c):
-            shape = (rows, stay.shape[1])
-            kept = lax.dynamic_slice(stay, (at_c * rows, 0), shape)
-            late = lax.dynamic_slice(arrived, (at_c * rows, 0), shape)
-            return (kept + late.astype(jnp.float32)).astype(jnp.bfloat16)
-
-        own_blocks.append(done(c))
-        other_blocks.append(swap(done(1 - c), "grp", 1))
-    return place_columns(place, groups, own_blocks, other_blocks, out_columns)
+        arrived[partner] = (swap(leave, "seg", 1), over)
+    terms = []
+    for group, (stay, stay_far) in zip(groups, kept):
+        leave, leave_far = arrived[group[0]]
+        terms += [stay, leave, stay_far, leave_far]
+    return place_columns(place, groups, terms, out_columns)
 
 
 def solution(mesh):

time: 337 us -> 327 us (0.970)
  waiting for transfers between devices: 170 us -> 164 us
  other arithmetic: 13.6 us -> 8.73 us
    ppermute x45, waiting for transfers between devices: 170 us -> 163 us  [swap(): return lax.ppermute(value, axis, [(i, i ^ bit) for i in range(count)])]
    pallas_call x2 -> x3, Pallas kernels: 9.83 us -> 13.6 us  [mix_near(): pl.pallas_call(kernel, grid=(4,), out_shape=jax.ShapeDtypeStruct((tokens_...]
    ppermute x0 -> x3, starting transfers between devices: none -> 3.47 us  [folded(): over = lax.ppermute(leave_far, ('grp', 'seg'), crossed)]
  transfers between devices with their start and end apart: 45 -> 48, of which waited for: 17 -> 15; matrix products, arithmetic and copies ran while one was open for 6% -> 5% of each run, Pallas kernels for 22% -> 25%
where the time goes in v1:
time: 327 us; the launch traced here: 326 us
  waiting for transfers between devices  164 us (50%)
  Pallas kernels  84.1 us (26%)
  starting transfers between devices  55.7 us (17%)
  local copies, waits for them, and re-layouts  12.7 us (4%)
  other arithmetic  8.73 us (3%)
    ppermute x45, waiting for transfers between devices, swap(): return lax.ppermute(value, axis, [(i, i ^ bit) for i in range(count)])  163 us
    ppermute x45, starting transfers between devices, swap(): return lax.ppermute(value, axis, [(i, i ^ bit) for i in range(count)])  52.2 us
    pallas_call x4, Pallas kernels, project(): pl.pallas_call(kernel, grid=(tokens_here // rows,), out_shape=out_shape,...  26.4 us
    pallas_call x3, Pallas kernels, mix_near(): pl.pallas_call(kernel, grid=(4,), out_shape=jax.ShapeDtypeStruct((tokens_...  13.6 us
    pallas_call x3, Pallas kernels, mix_far(): pl.pallas_call(kernel, grid_spec=grid_spec, out_shape=[jax.ShapeDtypeStru...  13.4 us
    pallas_call x1, Pallas kernels, run_gates(): pl.pallas_call(kernel, grid_spec=grid_spec, out_shape=[jax.ShapeDtypeStru...  11.2 us
    pallas_call x1, Pallas kernels, run_states(): pl.pallas_call(kernel, grid_spec=grid_spec, out_shape=jax.ShapeDtypeStruc...  8.42 us
    pallas_call x1, Pallas kernels, assemble(): pl.pallas_call(kernel, out_shape=jax.ShapeDtypeStruct((2 * lows * rows, 2...  8.17 us
  transfers between devices with their start and end apart: 48, of which 15 were waited for; matrix products, arithmetic and copies ran while one was open for 5% of the time, Pallas kernels for 25%

profile of v1, /device:TPU:0, one launch (start us, length us, event | category | flops | bytes accessed | tf_op | source)
XLA Modules:
  0.0 325.9 jit_solution(3505328675859405904)
XLA Ops:
  0.0 3.1 collective-permute-start.1
  3.1 2.5 constant_dynamic-slice_fusion.2
  8.5 1.5 collective-permute-start
  10.1 16.4 %collective-permute-done.1.refs_2_ = bf16[256,2048]{1,0:T(8,128)(2,1)S(1)} collective-permute-done((bf16[256,2048]{1,0:T(8,128)(2,1)}, bf16[256,2048]{1,0:T(8,128)(2,1)S(1)}, u32[]{:S(2)}, u32[]{:S(2)}) %collective-permute-start.1) | collective-permute-done | bytes 1048608 | tf_op jit(solution)/shard_map/ppermute | solution.py:122
  26.4 1.7 collective-permute-start.2
  29.4 1.6 collective-permute-start.17
  31.1 2.7 collective-permute-start.19
  34.6 20.0 %collective-permute-done.17.refs_1_ = bf16[512,512]{1,0:T(8,128)(2,1)} collective-permute-done((bf16[512,512]{1,0:T(8,128)(2,1)S(1)}, bf16[512,512]{1,0:T(8,128)(2,1)}, u32[]{:S(2)}, u32[]{:S(2)}) %collective-permute-start.17) | collective-permute-done | bytes 524320 | tf_op jit(solution)/shard_map/ppermute | solution.py:122
  54.6 1.5 collective-permute-done.2.refs_3_
  56.2 13.2 %collective-permute-done.19.refs_2_ = bf16[512,512]{1,0:T(8,128)(2,1)} collective-permute-done((bf16[512,512]{1,0:T(8,128)(2,1)S(1)}, bf16[512,512]{1,0:T(8,128)(2,1)}, u32[]{:S(2)}, u32[]{:S(2)}) %collective-permute-start.19) | collective-permute-done | bytes 524320 | tf_op jit(solution)/shard_map/ppermute | solution.py:122
  69.4 1.5 collective-permute-start.16
  70.9 10.6 %collective-permute-start.11 = (bf16[512,512]{1,0:T(8,128)(2,1)S(1)}, bf16[512,512]{1,0:T(8,128)(2,1)S(1)}, u32[]{:S(2)}, u32[]{:S(2)}) collective-permute-start(bf16[512,512]{1,0:T(8,128)(2,1)S(1)} %pad_maximum_fusion.1.refs_0_), channel_id=1, source_target_pairs={{0,4},{2,6},{4,0},{6,2},{1,5},{3,7},{5,1},{7,3},{8,12},{10,14},{12... | collective-permute-start | bytes 1572872 | tf_op jit(solution)/shard_map/ppermute | solution.py:122
  82.4 1.9 collective-permute-start.13
  84.3 32.2 %collective-permute-done.11.refs_2_ = bf16[512,512]{1,0:T(8,128)(2,1)S(1)} collective-permute-done((bf16[512,512]{1,0:T(8,128)(2,1)S(1)}, bf16[512,512]{1,0:T(8,128)(2,1)S(1)}, u32[]{:S(2)}, u32[]{:S(2)}) %collective-permute-start.11) | collective-permute-done | bytes 524320 | tf_op jit(solution)/shard_map/ppermute | solution.py:122
  116.6 1.6 collective-permute-start.18
  121.9 8.2 %set_together.1.source_ref = bf16[1024,4096]{1,0:T(8,128)(2,1)} custom-call(s32[7]{0:T(128)} %stack.89.place_ref, bf16[256,2048]{1,0:T(8,128)(2,1)} %refs_0_.1, bf16[256,2048]{1,0:T(8,128)(2,1)} %copy-done.8, bf16[256,2048]{1,0:T(8,128)(2,1)} %copy-done.6, bf16[256,2048]{1,0:T(8,128)(2,1)} %copy-done.9, bf16[256,2048]{1,0:T(8,128)(2,1)} %copy-done.7, ...), custom_call_target="tpu_custom_call" | custom-call | bytes 16777216 | tf_op jit(solution)/shard_map/set_together/pallas_call | solution.py:151
  130.1 6.5 %project.5.refs_4_ = f32[1024,512]{1,0:T(8,128)} custom-call(bf16[1024,4096]{1,0:T(8,128)(2,1)} %set_together.1.source_ref, bf16[512,512]{1,0:T(8,128)(2,1)} %copy-done.4, bf16[512,512]{1,0:T(8,128)(2,1)} %collective-permute-done.17.refs_1_, bf16[512,512]{1,0:T(8,128)(2,1)} %collective-permute-done.19.refs_2_, bf16[512,512]{1,0:T(8,128)(2,1)} %collective-permute-done.21.refs_3_), custom_call_target="tpu_custom_call" | custom-call | flops 2147483648 | bytes 6291456 | tf_op jit(solution)/shard_map/project/pallas_call | solution.py:228
  139.6 3.3 %collective-permute-done.20.refs_2_ = bf16[512,512]{1,0:T(8,128)(2,1)S(1)} collective-permute-done((bf16[512,512]{1,0:T(8,128)(2,1)}, bf16[512,512]{1,0:T(8,128)(2,1)S(1)}, u32[]{:S(2)}, u32[]{:S(2)}) %collective-permute-start.20) | collective-permute-done | bytes 524320 | tf_op jit(solution)/shard_map/ppermute | solution.py:122
  142.9 1.5 collective-permute-start.14
  144.4 9.8 %collective-permute-done.22.refs_3_ = bf16[512,512]{1,0:T(8,128)(2,1)} collective-permute-done((bf16[512,512]{1,0:T(8,128)(2,1)}, bf16[512,512]{1,0:T(8,128)(2,1)}, u32[]{:S(2)}, u32[]{:S(2)}) %collective-permute-start.22) | collective-permute-done | bytes 524320 | tf_op jit(solution)/shard_map/ppermute | solution.py:122
  154.2 6.5 %project.6.x_ref = bf16[1024,512]{1,0:T(8,128)(2,1)} custom-call(bf16[1024,4096]{1,0:T(8,128)(2,1)} %set_together.1.source_ref, bf16[512,512]{1,0:T(8,128)(2,1)} %copy-done.24, bf16[512,512]{1,0:T(8,128)(2,1)} %copy-done.25, bf16[512,512]{1,0:T(8,128)(2,1)} %copy-done.26, bf16[512,512]{1,0:T(8,128)(2,1)} %collective-permute-done.22.refs_3_, ...), custom_call_target="tpu_custom_call" | custom-call | flops 2147483648 | bytes 6291456 | tf_op jit(solution)/shard_map/project/pallas_call | solution.py:228
  160.7 11.2 %gates.1 = (f32[4,1024,128]{2,1,0:T(8,128)}, f32[4,1024,128]{2,1,0:T(8,128)}, f32[2,24,512]{2,1,0:T(8,128)}, f32[2,16,512]{2,1,0:T(8,128)}) custom-call(s32[7]{0:T(128)} %stack.89.place_ref, bf16[1024,512]{1,0:T(8,128)(2,1)} %project.6.x_ref, f32[16,2048]{1,0:T(8,128)} %stack.102.table_ref, bf16[8,256,256]{2,1,0:T(8,128)(2,1)} %decay_w.3, ...), custom_call_target="tpu_custom_call" | custom-call | flops 536870912 | bytes 5242880 | tf_op jit(solution)/shard_map/gates/pallas_call | solution.py:361
  171.9 2.1 collective-permute-start.23
  174.9 2.5 collective-permute-done.23
  177.4 1.6 collective-permute-start.24
  179.0 6.3 %project.4.refs_4_ = f32[1024,512]{1,0:T(8,128)} custom-call(bf16[1024,4096]{1,0:T(8,128)(2,1)} %set_together.1.source_ref, bf16[512,512]{1,0:T(8,128)(2,1)} %copy-done.3, bf16[512,512]{1,0:T(8,128)(2,1)} %collective-permute-done.9.refs_1_, bf16[512,512]{1,0:T(8,128)(2,1)} %copy-done.15, bf16[512,512]{1,0:T(8,128)(2,1)} %collective-permute-done.13.refs_3_), custom_call_target="tpu_custom_call" | custom-call | flops 2147483648 | bytes 6291456 | tf_op jit(solution)/shard_map/project/pallas_call | solution.py:228
  185.2 13.5 %collective-permute-done.24 = f32[2,2,16,512]{3,2,1,0:T(8,128)S(1)} collective-permute-done((f32[2,2,16,512]{3,2,1,0:T(8,128)S(1)}, f32[2,2,16,512]{3,2,1,0:T(8,128)S(1)}, u32[]{:S(2)}, u32[]{:S(2)}) %collective-permute-start.24) | collective-permute-done | bytes 131104 | tf_op jit(solution)/shard_map/ppermute | solution.py:122
  200.6 8.4 %states.1.refs_5_ = f32[4,1024,128]{2,1,0:T(8,128)} custom-call(s32[7]{0:T(128)} %stack.89.place_ref, f32[4,1024,128]{2,1,0:T(8,128)} %get-tuple-element.25.decay_ref, f32[4,1024,128]{2,1,0:T(8,128)} %get-tuple-element.26.drive_ref, f32[2,24,512]{2,1,0:T(8,128)} %get-tuple-element.27.part_ref, f32[8,16,512]{2,1,0:T(8,128)} %bitcast.39, ...), custom_call_target="tpu_custom_call" | custom-call | flops 5242880 | bytes 6291456 | tf_op jit(solution)/shard_map/states/pallas_call | solution.py:520
  211.0 7.2 %project.7.refs_0_ = bf16[1024,512]{1,0:T(8,128)(2,1)} custom-call(bf16[1024,4096]{1,0:T(8,128)(2,1)} %set_together.1.source_ref, bf16[512,512]{1,0:T(8,128)(2,1)} %copy-done.17, bf16[512,512]{1,0:T(8,128)(2,1)} %copy-done.18, bf16[512,512]{1,0:T(8,128)(2,1)} %copy-done.19, bf16[512,512]{1,0:T(8,128)(2,1)} %copy-done.20, f32[1024,512]{1,0:T(8,128)} %project.4.refs_4_, ...), custom_call_target="tpu_custom_call" | custom-call | flops 2147483648 | bytes 6291456 | tf_op jit(solution)/shard_map/project/pallas_call | solution.py:228
  218.7 2.0 collective-permute-start.36
  220.7 1.5 collective-permute-start.27
  223.9 20.3 %collective-permute-done.36 = bf16[1024,256]{1,0:T(8,128)(2,1)S(1)} collective-permute-done((bf16[1024,256]{1,0:T(8,128)(2,1)S(1)}, bf16[1024,256]{1,0:T(8,128)(2,1)S(1)}, u32[]{:S(2)}, u32[]{:S(2)}) %collective-permute-start.36) | collective-permute-done | bytes 524320 | tf_op jit(solution)/shard_map/ppermute | solution.py:122
  244.3 1.5 collective-permute-start.37
  245.8 2.0 broadcast_select_fusion.5
  248.8 2.3 broadcast_select_fusion
  251.0 8.0 %collective-permute-done.37 = bf16[1024,256]{1,0:T(8,128)(2,1)S(1)} collective-permute-done((bf16[1024,256]{1,0:T(8,128)(2,1)S(1)}, bf16[1024,256]{1,0:T(8,128)(2,1)S(1)}, u32[]{:S(2)}, u32[]{:S(2)}) %collective-permute-start.37) | collective-permute-done | bytes 524320 | tf_op jit(solution)/shard_map/ppermute | solution.py:122
  260.4 8.0 %collective-permute-done.30 = bf16[1024,256]{1,0:T(8,128)(2,1)S(1)} collective-permute-done((bf16[1024,256]{1,0:T(8,128)(2,1)S(1)}, bf16[1024,256]{1,0:T(8,128)(2,1)S(1)}, u32[]{:S(2)}, u32[]{:S(2)}) %collective-permute-start.30) | collective-permute-done | bytes 524320 | tf_op jit(solution)/shard_map/ppermute | solution.py:122
  269.8 1.5 collective-permute-start.31
  271.4 4.3 %mix_near.5 = f32[1024,256]{1,0:T(8,128)} custom-call(s32[7]{0:T(128)} %stack.89.place_ref, bf16[1024,512]{1,0:T(8,128)(2,1)} %project.7.refs_0_, bf16[1024,512]{1,0:T(8,128)(2,1)} %copy-done.2, bf16[1024,256]{1,0:T(8,128)(2,1)} %get-tuple-element.41.refs_2_), custom_call_target="tpu_custom_call" | custom-call | flops 536870912 | bytes 3145728 | tf_op jit(solution)/shard_map/mix_near/pallas_call | solution.py:560
  275.7 4.3 %mix_near.4 = f32[1024,256]{1,0:T(8,128)} custom-call(s32[7]{0:T(128)} %stack.89.place_ref, bf16[1024,512]{1,0:T(8,128)(2,1)} %project.7.refs_0_, bf16[1024,512]{1,0:T(8,128)(2,1)} %copy-done.2, bf16[1024,256]{1,0:T(8,128)(2,1)} %get-tuple-element.43.refs_2_), custom_call_target="tpu_custom_call" | custom-call | flops 536870912 | bytes 3145728 | tf_op jit(solution)/shard_map/mix_near/pallas_call | solution.py:560
  280.0 5.0 %mix_near.3 = f32[1024,512]{1,0:T(8,128)} custom-call(s32[7]{0:T(128)} %stack.89.place_ref, bf16[1024,512]{1,0:T(8,128)(2,1)} %project.7.refs_0_, bf16[1024,512]{1,0:T(8,128)(2,1)} %copy-done.2, bf16[1024,256]{1,0:T(8,128)(2,1)} %get-tuple-element.47.refs_2_, bf16[1024,256]{1,0:T(8,128)(2,1)} %get-tuple-element.45.refs_3_), custom_call_target="tpu_custom_call" | custom-call | flops 1073741824 | bytes 4194304 | tf_op jit(solution)/shard_map/mix_near/pallas_call | solution.py:560
  286.1 4.1 %mix_far.5 = (bf16[256,256]{1,0:T(8,128)(2,1)}, bf16[256,256]{1,0:T(8,128)(2,1)}, f32[256,256]{1,0:T(8,128)}, bf16[256,256]{1,0:T(8,128)(2,1)}) custom-call(s32[7]{0:T(128)} %stack.89.place_ref, bf16[2,2,256,512]{3,2,1,0:T(8,128)(2,1)} %bitcast.30, bf16[2,2,256,512]{3,2,1,0:T(8,128)(2,1)} %bitcast.33, bf16[1024,256]{1,0:T(8,128)(2,1)} %copy-done.22, ...), custom_call_target="tpu_custom_call" | custom-call | flops 536870912 | bytes 3932160 | tf_op jit(solution)/shard_map/mix_far/pallas_call | solution.py:627
  290.3 2.1 collective-permute-start.46
  292.4 4.1 %mix_far.4 = (bf16[256,256]{1,0:T(8,128)(2,1)}, bf16[256,256]{1,0:T(8,128)(2,1)}, f32[256,256]{1,0:T(8,128)}, bf16[256,256]{1,0:T(8,128)(2,1)}) custom-call(s32[7]{0:T(128)} %stack.89.place_ref, bf16[2,2,256,512]{3,2,1,0:T(8,128)(2,1)} %bitcast.31, bf16[2,2,256,512]{3,2,1,0:T(8,128)(2,1)} %bitcast.34, bf16[1024,256]{1,0:T(8,128)(2,1)} %copy-done.21, ...), custom_call_target="tpu_custom_call" | custom-call | flops 536870912 | bytes 3932160 | tf_op jit(solution)/shard_map/mix_far/pallas_call | solution.py:627
  298.1 5.3 %mix_far.3 = (bf16[256,512]{1,0:T(8,128)(2,1)}, bf16[256,512]{1,0:T(8,128)(2,1)}, f32[256,512]{1,0:T(8,128)}, bf16[256,512]{1,0:T(8,128)(2,1)}) custom-call(s32[7]{0:T(128)} %stack.89.place_ref, bf16[2,2,256,512]{3,2,1,0:T(8,128)(2,1)} %bitcast.32, bf16[2,2,256,512]{3,2,1,0:T(8,128)(2,1)} %bitcast.35, bf16[1024,256]{1,0:T(8,128)(2,1)} %collective-permute-done.28.refs_2_, ...), custom_call_target="tpu_custom_call" | custom-call | flops 1073741824 | bytes 5767168 | tf_op jit(solution)/shard_map/mix_far/pallas_call | solution.py:627
  303.6 2.0 collective-permute-start.35
  307.2 14.1 %collective-permute-done.45.refs_9_ = bf16[256,256]{1,0:T(8,128)(2,1)S(1)} collective-permute-done((bf16[256,256]{1,0:T(8,128)(2,1)S(1)}, bf16[256,256]{1,0:T(8,128)(2,1)S(1)}, u32[]{:S(2)}, u32[]{:S(2)}) %collective-permute-start.45) | collective-permute-done | bytes 131104 | tf_op jit(solution)/shard_map/ppermute | solution.py:122
  323.1 2.8 place.1
  (172 shorter events, 29.9 us)
Async XLA Ops:
  0.0 26.4 %collective-permute-start.1 = (bf16[256,2048]{1,0:T(8,128)(2,1)}, bf16[256,2048]{1,0:T(8,128)(2,1)S(1)}, u32[]{:S(2)}, u32[]{:S(2)}) collective-permute-start(bf16[256,2048]{1,0:T(8,128)(2,1)} %refs_0_.1), channel_id=1, source_target_pairs={{0,2},{2,0},{4,6},{6,4},{1,3},{3,1},{5,7},{7,5},{8,10},{10,8},{12,... | collective-permute-start | bytes 3145736 | tf_op jit(solution)/shard_map/ppermute | solution.py:122
  6.4 21.8 %collective-permute-start.15 = (bf16[512,512]{1,0:T(8,128)(2,1)}, bf16[512,512]{1,0:T(8,128)(2,1)}, u32[]{:S(2)}, u32[]{:S(2)}) collective-permute-start(bf16[512,512]{1,0:T(8,128)(2,1)} %pad_maximum_fusion.3), channel_id=1, source_target_pairs={{0,8},{8,0},{16,24},{24,16},{1,9},{9,1},{17,25},{25,17},{2,10},{10... | collective-permute-start | bytes 1572872 | tf_op jit(solution)/shard_map/ppermute | solution.py:122
  8.0 25.7 %collective-permute-start.3 = (bf16[256,2048]{1,0:T(8,128)(2,1)S(1)}, bf16[256,2048]{1,0:T(8,128)(2,1)S(1)}, u32[]{:S(2)}, u32[]{:S(2)}) collective-permute-start(bf16[256,2048]{1,0:T(8,128)(2,1)S(1)} %copy-done.5), channel_id=1, source_target_pairs={{0,8},{8,0},{16,24},{24,16},{1,9},{9,1},{17,25},{25,17},{2,10},{10... | collective-permute-start | bytes 3145736 | tf_op jit(solution)/shard_map/ppermute | solution.py:122
  8.5 26.0 %collective-permute-start = (bf16[256,2048]{1,0:T(8,128)(2,1)S(1)}, bf16[256,2048]{1,0:T(8,128)(2,1)S(1)}, u32[]{:S(2)}, u32[]{:S(2)}) collective-permute-start(bf16[256,2048]{1,0:T(8,128)(2,1)S(1)} %copy-done.5), channel_id=1, source_target_pairs={{0,1},{1,0},{2,3},{3,2},{4,5},{5,4},{6,7},{7,6},{8,9},{9,8},{10,11... | collective-permute-start | bytes 3145736 | tf_op jit(solution)/shard_map/ppermute | solution.py:122
  26.4 29.7 %collective-permute-start.2 = (bf16[256,2048]{1,0:T(8,128)(2,1)S(1)}, bf16[256,2048]{1,0:T(8,128)(2,1)S(1)}, u32[]{:S(2)}, u32[]{:S(2)}) collective-permute-start(bf16[256,2048]{1,0:T(8,128)(2,1)S(1)} %collective-permute-done.1.refs_2_), channel_id=1, source_target_pairs={{0,1},{1,0},{2,3},{3,2},{4,5},{5,4},{6,7},{7,6},{8,9},{9,8},{10,11... | collective-permute-start | bytes 3145736 | tf_op jit(solution)/shard_map/ppermute | solution.py:122
  28.2 2.9 collective-permute-start.7
  29.4 25.2 %collective-permute-start.17 = (bf16[512,512]{1,0:T(8,128)(2,1)S(1)}, bf16[512,512]{1,0:T(8,128)(2,1)}, u32[]{:S(2)}, u32[]{:S(2)}) collective-permute-start(bf16[512,512]{1,0:T(8,128)(2,1)S(1)} %pad_maximum_fusion.5), channel_id=1, source_target_pairs={{0,2},{2,0},{4,6},{6,4},{1,3},{3,1},{5,7},{7,5},{8,10},{10,8},{12,... | collective-permute-start | bytes 1572872 | tf_op jit(solution)/shard_map/ppermute | solution.py:122
  31.1 38.4 %collective-permute-start.19 = (bf16[512,512]{1,0:T(8,128)(2,1)S(1)}, bf16[512,512]{1,0:T(8,128)(2,1)}, u32[]{:S(2)}, u32[]{:S(2)}) collective-permute-start(bf16[512,512]{1,0:T(8,128)(2,1)S(1)} %pad_maximum_fusion.4.refs_0_), channel_id=1, source_target_pairs={{0,4},{2,6},{4,0},{6,2},{1,5},{3,7},{5,1},{7,3},{8,12},{10,14},{12... | collective-permute-start | bytes 1572872 | tf_op jit(solution)/shard_map/ppermute | solution.py:122
  33.7 37.2 %collective-permute-start.21 = (bf16[512,512]{1,0:T(8,128)(2,1)S(1)}, bf16[512,512]{1,0:T(8,128)(2,1)}, u32[]{:S(2)}, u32[]{:S(2)}) collective-permute-start(bf16[512,512]{1,0:T(8,128)(2,1)S(1)} %pad_maximum_fusion.5), channel_id=1, source_target_pairs={{0,6},{2,4},{4,2},{6,0},{1,7},{3,5},{5,3},{7,1},{8,14},{10,12},{12... | collective-permute-start | bytes 1572872 | tf_op jit(solution)/shard_map/ppermute | solution.py:122
  34.6 82.0 %collective-permute-start.5 = (bf16[256,2048]{1,0:T(8,128)(2,1)S(1)}, bf16[256,2048]{1,0:T(8,128)(2,1)S(1)}, u32[]{:S(2)}, u32[]{:S(2)}) collective-permute-start(bf16[256,2048]{1,0:T(8,128)(2,1)S(1)} %collective-permute-done.1.refs_2_), channel_id=1, source_target_pairs={{0,8},{8,0},{16,24},{24,16},{1,9},{9,1},{17,25},{25,17},{2,10},{10... | collective-permute-start | bytes 3145736 | tf_op jit(solution)/shard_map/ppermute | solution.py:122
  54.6 63.6 %collective-permute-start.4 = (bf16[256,2048]{1,0:T(8,128)(2,1)S(1)}, bf16[256,2048]{1,0:T(8,128)(2,1)S(1)}, u32[]{:S(2)}, u32[]{:S(2)}) collective-permute-start(bf16[256,2048]{1,0:T(8,128)(2,1)S(1)} %collective-permute-done.refs_1_), channel_id=1, source_target_pairs={{0,8},{8,0},{16,24},{24,16},{1,9},{9,1},{17,25},{25,17},{2,10},{10... | collective-permute-start | bytes 3145736 | tf_op jit(solution)/shard_map/ppermute | solution.py:122
  56.1 62.7 %collective-permute-start.6 = (bf16[256,2048]{1,0:T(8,128)(2,1)S(1)}, bf16[256,2048]{1,0:T(8,128)(2,1)S(1)}, u32[]{:S(2)}, u32[]{:S(2)}) collective-permute-start(bf16[256,2048]{1,0:T(8,128)(2,1)S(1)} %collective-permute-done.2.refs_3_), channel_id=1, source_target_pairs={{0,8},{8,0},{16,24},{24,16},{1,9},{9,1},{17,25},{25,17},{2,10},{10... | collective-permute-start | bytes 3145736 | tf_op jit(solution)/shard_map/ppermute | solution.py:122
  69.4 13.0 %collective-permute-start.16 = (bf16[512,512]{1,0:T(8,128)(2,1)S(1)}, bf16[512,512]{1,0:T(8,128)(2,1)S(1)}, u32[]{:S(2)}, u32[]{:S(2)}) collective-permute-start(bf16[512,512]{1,0:T(8,128)(2,1)S(1)} %pad_maximum_fusion.4.refs_0_), channel_id=1, source_target_pairs={{0,16},{8,24},{16,0},{24,8},{1,17},{9,25},{17,1},{25,9},{2,18},{10... | collective-permute-start | bytes 1572872 | tf_op jit(solution)/shard_map/ppermute | solution.py:122
  70.9 45.6 %collective-permute-start.11 = (bf16[512,512]{1,0:T(8,128)(2,1)S(1)}, bf16[512,512]{1,0:T(8,128)(2,1)S(1)}, u32[]{:S(2)}, u32[]{:S(2)}) collective-permute-start(bf16[512,512]{1,0:T(8,128)(2,1)S(1)} %pad_maximum_fusion.1.refs_0_), channel_id=1, source_target_pairs={{0,4},{2,6},{4,0},{6,2},{1,5},{3,7},{5,1},{7,3},{8,12},{10,14},{12... | collective-permute-start | bytes 1572872 | tf_op jit(solution)/shard_map/ppermute | solution.py:122
  82.4 54.1 %collective-permute-start.13 = (bf16[512,512]{1,0:T(8,128)(2,1)}, bf16[512,512]{1,0:T(8,128)(2,1)}, u32[]{:S(2)}, u32[]{:S(2)}) collective-permute-start(bf16[512,512]{1,0:T(8,128)(2,1)} %pad_maximum_fusion.2), channel_id=1, source_target_pairs={{0,6},{2,4},{4,2},{6,0},{1,7},{3,5},{5,3},{7,1},{8,14},{10,12},{12... | collective-permute-start | bytes 1572872 | tf_op jit(solution)/shard_map/ppermute | solution.py:122
  116.6 20.9 %collective-permute-start.9 = (bf16[512,512]{1,0:T(8,128)(2,1)}, bf16[512,512]{1,0:T(8,128)(2,1)}, u32[]{:S(2)}, u32[]{:S(2)}) collective-permute-start(bf16[512,512]{1,0:T(8,128)(2,1)} %pad_maximum_fusion.2), channel_id=1, source_target_pairs={{0,2},{2,0},{4,6},{6,4},{1,3},{3,1},{5,7},{7,5},{8,10},{10,8},{12,... | collective-permute-start | bytes 1572872 | tf_op jit(solution)/shard_map/ppermute | solution.py:122
  116.6 22.1 %collective-permute-start.18 = (bf16[512,512]{1,0:T(8,128)(2,1)}, bf16[512,512]{1,0:T(8,128)(2,1)S(1)}, u32[]{:S(2)}, u32[]{:S(2)}) collective-permute-start(bf16[512,512]{1,0:T(8,128)(2,1)} %collective-permute-done.17.refs_1_), channel_id=1, source_target_pairs={{0,16},{8,24},{16,0},{24,8},{1,17},{9,25},{17,1},{25,9},{2,18},{10... | collective-permute-start | bytes 1572872 | tf_op jit(solution)/shard_map/ppermute | solution.py:122
  118.2 24.7 %collective-permute-start.20 = (bf16[512,512]{1,0:T(8,128)(2,1)}, bf16[512,512]{1,0:T(8,128)(2,1)S(1)}, u32[]{:S(2)}, u32[]{:S(2)}) collective-permute-start(bf16[512,512]{1,0:T(8,128)(2,1)} %collective-permute-done.19.refs_2_), channel_id=1, source_target_pairs={{0,16},{8,24},{16,0},{24,8},{1,17},{9,25},{17,1},{25,9},{2,18},{10... | collective-permute-start | bytes 1572872 | tf_op jit(solution)/shard_map/ppermute | solution.py:122
  120.1 34.1 %collective-permute-start.22 = (bf16[512,512]{1,0:T(8,128)(2,1)}, bf16[512,512]{1,0:T(8,128)(2,1)}, u32[]{:S(2)}, u32[]{:S(2)}) collective-permute-start(bf16[512,512]{1,0:T(8,128)(2,1)} %collective-permute-done.21.refs_3_), channel_id=1, source_target_pairs={{0,16},{8,24},{16,0},{24,8},{1,17},{9,25},{17,1},{25,9},{2,18},{10... | collective-permute-start | bytes 1572872 | tf_op jit(solution)/shard_map/ppermute | solution.py:122
  136.5 72.5 %collective-permute-start.8 = (bf16[512,512]{1,0:T(8,128)(2,1)S(1)}, bf16[512,512]{1,0:T(8,128)(2,1)S(1)}, u32[]{:S(2)}, u32[]{:S(2)}) collective-permute-start(bf16[512,512]{1,0:T(8,128)(2,1)S(1)} %pad_maximum_fusion.1.refs_0_), channel_id=1, source_target_pairs={{0,16},{8,24},{16,0},{24,8},{1,17},{9,25},{17,1},{25,9},{2,18},{10... | collective-permute-start | bytes 1572872 | tf_op jit(solution)/shard_map/ppermute | solution.py:122
  137.5 71.5 %collective-permute-start.10 = (bf16[512,512]{1,0:T(8,128)(2,1)}, bf16[512,512]{1,0:T(8,128)(2,1)S(1)}, u32[]{:S(2)}, u32[]{:S(2)}) collective-permute-start(bf16[512,512]{1,0:T(8,128)(2,1)} %collective-permute-done.9.refs_1_), channel_id=1, source_target_pairs={{0,16},{8,24},{16,0},{24,8},{1,17},{9,25},{17,1},{25,9},{2,18},{10... | collective-permute-start | bytes 1572872 | tf_op jit(solution)/shard_map/ppermute | solution.py:122
  138.6 70.4 %collective-permute-start.12 = (bf16[512,512]{1,0:T(8,128)(2,1)S(1)}, bf16[512,512]{1,0:T(8,128)(2,1)S(1)}, u32[]{:S(2)}, u32[]{:S(2)}) collective-permute-start(bf16[512,512]{1,0:T(8,128)(2,1)S(1)} %copy-done.16), channel_id=1, source_target_pairs={{0,16},{8,24},{16,0},{24,8},{1,17},{9,25},{17,1},{25,9},{2,18},{10... | collective-permute-start | bytes 1572872 | tf_op jit(solution)/shard_map/ppermute | solution.py:122
  142.9 66.2 %collective-permute-start.14 = (bf16[512,512]{1,0:T(8,128)(2,1)}, bf16[512,512]{1,0:T(8,128)(2,1)S(1)}, u32[]{:S(2)}, u32[]{:S(2)}) collective-permute-start(bf16[512,512]{1,0:T(8,128)(2,1)} %collective-permute-done.13.refs_3_), channel_id=1, source_target_pairs={{0,16},{8,24},{16,0},{24,8},{1,17},{9,25},{17,1},{25,9},{2,18},{10... | collective-permute-start | bytes 1572872 | tf_op jit(solution)/shard_map/ppermute | solution.py:122
  171.9 5.4 %collective-permute-start.23 = (f32[2,16,512]{2,1,0:T(8,128)}, f32[2,16,512]{2,1,0:T(8,128)S(1)}, u32[]{:S(2)}, u32[]{:S(2)}) collective-permute-start(f32[2,16,512]{2,1,0:T(8,128)} %get-tuple-element.28), channel_id=1, source_target_pairs={{0,4},{2,6},{4,0},{6,2},{1,5},{3,7},{5,1},{7,3},{8,12},{10,14},{12... | collective-permute-start | bytes 196616 | tf_op jit(solution)/shard_map/ppermute | solution.py:122
  177.4 21.3 %collective-permute-start.24 = (f32[2,2,16,512]{3,2,1,0:T(8,128)S(1)}, f32[2,2,16,512]{3,2,1,0:T(8,128)S(1)}, u32[]{:S(2)}, u32[]{:S(2)}) collective-permute-start(f32[2,2,16,512]{3,2,1,0:T(8,128)S(1)} %get-tuple-element.64), channel_id=1, source_target_pairs={{0,16},{8,24},{16,0},{24,8},{1,17},{9,25},{17,1},{25,9},{2,18},{10... | collective-permute-start | bytes 393224 | tf_op jit(solution)/shard_map/ppermute | solution.py:122
  198.7 24.7 %collective-permute-start.39 = (bf16[1024,256]{1,0:T(8,128)(2,1)}, bf16[1024,256]{1,0:T(8,128)(2,1)S(1)}, u32[]{:S(2)}, u32[]{:S(2)}) collective-permute-start(bf16[1024,256]{1,0:T(8,128)(2,1)} %get-tuple-element.49), channel_id=1, source_target_pairs={{0,6},{2,4},{4,2},{6,0},{1,7},{3,5},{5,3},{7,1},{8,14},{10,12},{12... | collective-permute-start | bytes 1572872 | tf_op jit(solution)/shard_map/ppermute | solution.py:122
  218.2 30.5 %collective-permute-start.25 = (bf16[1024,512]{1,0:T(8,128)(2,1)}, bf16[1024,512]{1,0:T(8,128)(2,1)S(1)}, u32[]{:S(2)}, u32[]{:S(2)}) collective-permute-start(bf16[1024,512]{1,0:T(8,128)(2,1)} %project.7.refs_0_), channel_id=1, source_target_pairs={{0,1},{1,0},{2,3},{3,2},{4,5},{5,4},{6,7},{7,6},{8,9},{9,8},{10,11... | collective-permute-start | bytes 3145736 | tf_op jit(solution)/shard_map/ppermute | solution.py:122
  218.7 25.5 %collective-permute-start.36 = (bf16[1024,256]{1,0:T(8,128)(2,1)S(1)}, bf16[1024,256]{1,0:T(8,128)(2,1)S(1)}, u32[]{:S(2)}, u32[]{:S(2)}) collective-permute-start(bf16[1024,256]{1,0:T(8,128)(2,1)S(1)} %get-tuple-element.50), channel_id=1, source_target_pairs={{0,4},{2,6},{4,0},{6,2},{1,5},{3,7},{5,1},{7,3},{8,12},{10,14},{12... | collective-permute-start | bytes 1572872 | tf_op jit(solution)/shard_map/ppermute | solution.py:122
  220.7 25.0 %collective-permute-start.27 = (bf16[1024,256]{1,0:T(8,128)(2,1)S(1)}, bf16[1024,256]{1,0:T(8,128)(2,1)}, u32[]{:S(2)}, u32[]{:S(2)}) collective-permute-start(bf16[1024,256]{1,0:T(8,128)(2,1)S(1)} %get-tuple-element.50), channel_id=1, source_target_pairs={{0,16},{8,24},{16,0},{24,8},{1,17},{9,25},{17,1},{25,9},{2,18},{10... | collective-permute-start | bytes 1572872 | tf_op jit(solution)/shard_map/ppermute | solution.py:122
  222.2 25.5 %collective-permute-start.29 = (bf16[1024,256]{1,0:T(8,128)(2,1)}, bf16[1024,256]{1,0:T(8,128)(2,1)S(1)}, u32[]{:S(2)}, u32[]{:S(2)}) collective-permute-start(bf16[1024,256]{1,0:T(8,128)(2,1)} %get-tuple-element.49), channel_id=1, source_target_pairs={{0,2},{2,0},{4,6},{6,4},{1,3},{3,1},{5,7},{7,5},{8,10},{10,8},{12,... | collective-permute-start | bytes 1572872 | tf_op jit(solution)/shard_map/ppermute | solution.py:122
  223.4 24.8 %collective-permute-start.40 = (bf16[1024,256]{1,0:T(8,128)(2,1)S(1)}, bf16[1024,256]{1,0:T(8,128)(2,1)}, u32[]{:S(2)}, u32[]{:S(2)}) collective-permute-start(bf16[1024,256]{1,0:T(8,128)(2,1)S(1)} %collective-permute-done.39), channel_id=1, source_target_pairs={{0,16},{8,24},{16,0},{24,8},{1,17},{9,25},{17,1},{25,9},{2,18},{10... | collective-permute-start | bytes 1572872 | tf_op jit(solution)/shard_map/ppermute | solution.py:122
  244.3 14.8 %collective-permute-start.37 = (bf16[1024,256]{1,0:T(8,128)(2,1)S(1)}, bf16[1024,256]{1,0:T(8,128)(2,1)S(1)}, u32[]{:S(2)}, u32[]{:S(2)}) collective-permute-start(bf16[1024,256]{1,0:T(8,128)(2,1)S(1)} %collective-permute-done.36), channel_id=1, source_target_pairs={{0,16},{8,24},{16,0},{24,8},{1,17},{9,25},{17,1},{25,9},{2,18},{10... | collective-permute-start | bytes 1572872 | tf_op jit(solution)/shard_map/ppermute | solution.py:122
  245.7 24.1 %collective-permute-start.32 = (bf16[1024,512]{1,0:T(8,128)(2,1)}, bf16[1024,512]{1,0:T(8,128)(2,1)S(1)}, u32[]{:S(2)}, u32[]{:S(2)}) collective-permute-start(bf16[1024,512]{1,0:T(8,128)(2,1)} %project.7.refs_0_), channel_id=1, source_target_pairs={{0,8},{8,0},{16,24},{24,16},{1,9},{9,1},{17,25},{25,17},{2,10},{10... | collective-permute-start | bytes 3145736 | tf_op jit(solution)/shard_map/ppermute | solution.py:122
  247.7 48.7 %collective-permute-start.28 = (bf16[1024,256]{1,0:T(8,128)(2,1)S(1)}, bf16[1024,256]{1,0:T(8,128)(2,1)}, u32[]{:S(2)}, u32[]{:S(2)}) collective-permute-start(bf16[1024,256]{1,0:T(8,128)(2,1)S(1)} %get-tuple-element.48), channel_id=1, source_target_pairs={{0,1},{1,0},{2,3},{3,2},{4,5},{5,4},{6,7},{7,6},{8,9},{9,8},{10,11... | collective-permute-start | bytes 1572872 | tf_op jit(solution)/shard_map/ppermute | solution.py:122
  248.2 20.2 %collective-permute-start.30 = (bf16[1024,256]{1,0:T(8,128)(2,1)S(1)}, bf16[1024,256]{1,0:T(8,128)(2,1)S(1)}, u32[]{:S(2)}, u32[]{:S(2)}) collective-permute-start(bf16[1024,256]{1,0:T(8,128)(2,1)S(1)} %collective-permute-done.29), channel_id=1, source_target_pairs={{0,16},{8,24},{16,0},{24,8},{1,17},{9,25},{17,1},{25,9},{2,18},{10... | collective-permute-start | bytes 1572872 | tf_op jit(solution)/shard_map/ppermute | solution.py:122
  248.7 36.3 %collective-permute-start.26 = (bf16[1024,512]{1,0:T(8,128)(2,1)S(1)}, bf16[1024,512]{1,0:T(8,128)(2,1)S(1)}, u32[]{:S(2)}, u32[]{:S(2)}) collective-permute-start(bf16[1024,512]{1,0:T(8,128)(2,1)S(1)} %collective-permute-done.25), channel_id=1, source_target_pairs={{0,8},{8,0},{16,24},{24,16},{1,9},{9,1},{17,25},{25,17},{2,10},{10... | collective-permute-start | bytes 3145736 | tf_op jit(solution)/shard_map/ppermute | solution.py:122
  259.0 26.0 %collective-permute-start.41 = (bf16[1024,256]{1,0:T(8,128)(2,1)S(1)}, bf16[1024,256]{1,0:T(8,128)(2,1)S(1)}, u32[]{:S(2)}, u32[]{:S(2)}) collective-permute-start(bf16[1024,256]{1,0:T(8,128)(2,1)S(1)} %get-tuple-element.42), channel_id=1, source_target_pairs={{0,1},{1,0},{2,3},{3,2},{4,5},{5,4},{6,7},{7,6},{8,9},{9,8},{10,11... | collective-permute-start | bytes 1572872 | tf_op jit(solution)/shard_map/ppermute | solution.py:122
  268.4 21.8 %collective-permute-start.38 = (bf16[1024,256]{1,0:T(8,128)(2,1)S(1)}, bf16[1024,256]{1,0:T(8,128)(2,1)S(1)}, u32[]{:S(2)}, u32[]{:S(2)}) collective-permute-start(bf16[1024,256]{1,0:T(8,128)(2,1)S(1)} %get-tuple-element.44), channel_id=1, source_target_pairs={{0,1},{1,0},{2,3},{3,2},{4,5},{5,4},{6,7},{7,6},{8,9},{9,8},{10,11... | collective-permute-start | bytes 1572872 | tf_op jit(solution)/shard_map/ppermute | solution.py:122
  269.8 27.4 %collective-permute-start.31 = (bf16[1024,256]{1,0:T(8,128)(2,1)S(1)}, bf16[1024,256]{1,0:T(8,128)(2,1)S(1)}, u32[]{:S(2)}, u32[]{:S(2)}) collective-permute-start(bf16[1024,256]{1,0:T(8,128)(2,1)S(1)} %get-tuple-element.46), channel_id=1, source_target_pairs={{0,1},{1,0},{2,3},{3,2},{4,5},{5,4},{6,7},{7,6},{8,9},{9,8},{10,11... | collective-permute-start | bytes 1572872 | tf_op jit(solution)/shard_map/ppermute | solution.py:122
  290.2 13.2 %collective-permute-start.42 = (bf16[256,256]{1,0:T(8,128)(2,1)}, bf16[256,256]{1,0:T(8,128)(2,1)S(1)}, u32[]{:S(2)}, u32[]{:S(2)}) collective-permute-start(bf16[256,256]{1,0:T(8,128)(2,1)} %get-tuple-element.34), channel_id=1, source_target_pairs={{0,2},{2,0},{4,6},{6,4},{1,3},{3,1},{5,7},{7,5},{8,10},{10,8},{12,... | collective-permute-start | bytes 393224 | tf_op jit(solution)/shard_map/ppermute | solution.py:122
  290.2 13.3 %collective-permute-start.44 = (bf16[256,256]{1,0:T(8,128)(2,1)}, bf16[256,256]{1,0:T(8,128)(2,1)S(1)}, u32[]{:S(2)}, u32[]{:S(2)}) collective-permute-start(bf16[256,256]{1,0:T(8,128)(2,1)} %get-tuple-element.36), channel_id=1, source_target_pairs={{0,10},{2,8},{4,14},{6,12},{8,2},{10,0},{12,6},{14,4},{16,26},{18,... | collective-permute-start | bytes 393224 | tf_op jit(solution)/shard_map/ppermute | solution.py:786
  290.3 15.3 %collective-permute-start.46 = (bf16[256,256]{1,0:T(8,128)(2,1)}, bf16[256,256]{1,0:T(8,128)(2,1)S(1)}, u32[]{:S(2)}, u32[]{:S(2)}) collective-permute-start(bf16[256,256]{1,0:T(8,128)(2,1)} %get-tuple-element.39), channel_id=1, source_target_pairs={{0,8},{8,0},{16,24},{24,16},{1,9},{9,1},{17,25},{25,17},{2,10},{10... | collective-permute-start | bytes 393224 | tf_op jit(solution)/shard_map/ppermute | solution.py:122
  296.4 9.3 %collective-permute-start.43 = (bf16[256,256]{1,0:T(8,128)(2,1)}, bf16[256,256]{1,0:T(8,128)(2,1)S(1)}, u32[]{:S(2)}, u32[]{:S(2)}) collective-permute-start(bf16[256,256]{1,0:T(8,128)(2,1)} %get-tuple-element.35), channel_id=1, source_target_pairs={{0,8},{8,0},{16,24},{24,16},{1,9},{9,1},{17,25},{25,17},{2,10},{10... | collective-permute-start | bytes 393224 | tf_op jit(solution)/shard_map/ppermute | solution.py:122
  303.4 18.7 %collective-permute-start.33 = (bf16[256,512]{1,0:T(8,128)(2,1)}, bf16[256,512]{1,0:T(8,128)(2,1)S(1)}, u32[]{:S(2)}, u32[]{:S(2)}) collective-permute-start(bf16[256,512]{1,0:T(8,128)(2,1)} %get-tuple-element.30), channel_id=1, source_target_pairs={{0,2},{2,0},{4,6},{6,4},{1,3},{3,1},{5,7},{7,5},{8,10},{10,8},{12,... | collective-permute-start | bytes 786440 | tf_op jit(solution)/shard_map/ppermute | solution.py:122
  303.5 18.7 %collective-permute-start.34 = (bf16[256,512]{1,0:T(8,128)(2,1)}, bf16[256,512]{1,0:T(8,128)(2,1)S(1)}, u32[]{:S(2)}, u32[]{:S(2)}) collective-permute-start(bf16[256,512]{1,0:T(8,128)(2,1)} %get-tuple-element.31), channel_id=1, source_target_pairs={{0,8},{8,0},{16,24},{24,16},{1,9},{9,1},{17,25},{25,17},{2,10},{10... | collective-permute-start | bytes 786440 | tf_op jit(solution)/shard_map/ppermute | solution.py:122
  303.6 18.6 %collective-permute-start.35 = (bf16[256,512]{1,0:T(8,128)(2,1)}, bf16[256,512]{1,0:T(8,128)(2,1)S(1)}, u32[]{:S(2)}, u32[]{:S(2)}) collective-permute-start(bf16[256,512]{1,0:T(8,128)(2,1)} %get-tuple-element.32), channel_id=1, source_target_pairs={{0,10},{2,8},{4,14},{6,12},{8,2},{10,0},{12,6},{14,4},{16,26},{18,... | collective-permute-start | bytes 786440 | tf_op jit(solution)/shard_map/ppermute | solution.py:786
  305.6 15.7 %collective-permute-start.45 = (bf16[256,256]{1,0:T(8,128)(2,1)S(1)}, bf16[256,256]{1,0:T(8,128)(2,1)S(1)}, u32[]{:S(2)}, u32[]{:S(2)}) collective-permute-start(bf16[256,256]{1,0:T(8,128)(2,1)S(1)} %copy-done.44), channel_id=1, source_target_pairs={{0,2},{2,0},{4,6},{6,4},{1,3},{3,1},{5,7},{7,5},{8,10},{10,8},{12,... | collective-permute-start | bytes 393224 | tf_op jit(solution)/shard_map/ppermute | solution.py:122
  305.7 16.4 %collective-permute-start.47 = (bf16[256,256]{1,0:T(8,128)(2,1)S(1)}, bf16[256,256]{1,0:T(8,128)(2,1)S(1)}, u32[]{:S(2)}, u32[]{:S(2)}) collective-permute-start(bf16[256,256]{1,0:T(8,128)(2,1)S(1)} %copy-done.43), channel_id=1, source_target_pairs={{0,10},{2,8},{4,14},{6,12},{8,2},{10,0},{12,6},{14,4},{16,26},{18,... | collective-permute-start | bytes 393224 | tf_op jit(solution)/shard_map/ppermute | solution.py:786
  (45 other events, 681.7 us)

commit v2 on v1

--- a/solution.py
+++ b/solution.py
@@ -174,7 +174,7 @@
     return total
 
 
-def project(source, half, pieces, edge=None, before=None, state=None, last=True, rows=256):
+def project(source, half, pieces, edge=None, before=None, state=None, last=True, rows=512):
     tokens_here = source.shape[0]
     depth = source.shape[1] // 2
     width = pieces[0].shape[1]
@@ -549,7 +549,7 @@
 def mix_near(place, parts, pieces):
     tokens_here, deep = parts[0].shape
     width = pieces[0].shape[1]
-    rows = tokens_here // 4
+    rows = tokens_here // 2
     count = len(pieces)
 
     def kernel(place_ref, *refs):
@@ -559,7 +559,7 @@
 
     return pl.pallas_call(
         kernel,
-        grid=(4,),
+        grid=(2,),
         out_shape=jax.ShapeDtypeStruct((tokens_here, count * width), jnp.float32),
         in_specs=[SMEM]
         + [pl.BlockSpec((rows, deep), lambda i: (i, 0))] * 2
@@ -568,7 +568,7 @@
         compiler_params=pltpu.CompilerParams(vmem_limit_bytes=GRANT),
         cost_estimate=pl.CostEstimate(
             flops=4 * count * tokens_here * deep * width,
-            bytes_accessed=4 * tokens_here * deep + 16 * count * rows * width,
+            bytes_accessed=4 * tokens_here * deep + 8 * count * rows * width,
             transcendentals=0,
         ),
         name="mix_near",

time: 327 us -> 325 us (level)
  Pallas kernels: 84.1 us -> 78.3 us
  waiting for transfers between devices: 164 us -> 168 us
    ppermute x45, waiting for transfers between devices: 163 us -> 168 us  [swap(): return lax.ppermute(value, axis, [(i, i ^ bit) for i in range(count)])]
    pallas_call x3, Pallas kernels: 13.6 us -> 10.3 us  [mix_near(): pl.pallas_call(kernel, grid=(2,), out_shape=jax.ShapeDtypeStruct((tokens_...]
  transfers between devices with their start and end apart: 48 -> 48, of which waited for: 15 -> 15; matrix products, arithmetic and copies ran while one was open for 5% -> 5% of each run, Pallas kernels for 25% -> 23%
where the time goes in v2:
time: 325 us; the launch traced here: 324 us
  waiting for transfers between devices  168 us (52%)
  Pallas kernels  78.3 us (24%)
  starting transfers between devices  55.6 us (17%)
  local copies, waits for them, and re-layouts  12.7 us (4%)
  other arithmetic  8.73 us (3%)
    ppermute x45, waiting for transfers between devices, swap(): return lax.ppermute(value, axis, [(i, i ^ bit) for i in range(count)])  168 us
    ppermute x45, starting transfers between devices, swap(): return lax.ppermute(value, axis, [(i, i ^ bit) for i in range(count)])  52.2 us
    pallas_call x4, Pallas kernels, project(): pl.pallas_call(kernel, grid=(tokens_here // rows,), out_shape=out_shape,...  23.9 us
    pallas_call x3, Pallas kernels, mix_far(): pl.pallas_call(kernel, grid_spec=grid_spec, out_shape=[jax.ShapeDtypeStru...  13.4 us
    pallas_call x1, Pallas kernels, run_gates(): pl.pallas_call(kernel, grid_spec=grid_spec, out_shape=[jax.ShapeDtypeStru...  11.2 us
    pallas_call x3, Pallas kernels, mix_near(): pl.pallas_call(kernel, grid=(2,), out_shape=jax.ShapeDtypeStruct((tokens_...  10.3 us
    pallas_call x1, Pallas kernels, run_states(): pl.pallas_call(kernel, grid_spec=grid_spec, out_shape=jax.ShapeDtypeStruc...  8.42 us
    pallas_call x1, Pallas kernels, assemble(): pl.pallas_call(kernel, out_shape=jax.ShapeDtypeStruct((2 * lows * rows, 2...  8.17 us
  transfers between devices with their start and end apart: 48, of which 15 were waited for; matrix products, arithmetic and copies ran while one was open for 5% of the time, Pallas kernels for 23%

profile of v2, /device:TPU:0, one launch (start us, length us, event | category | flops | bytes accessed | tf_op | source)
XLA Modules:
  0.0 323.5 jit_solution(7778884132766855111)
XLA Ops:
  0.0 3.1 collective-permute-start.1
  3.1 2.5 constant_dynamic-slice_fusion.2
  8.5 1.5 collective-permute-start
  10.1 16.4 %collective-permute-done.1.refs_2_ = bf16[256,2048]{1,0:T(8,128)(2,1)S(1)} collective-permute-done((bf16[256,2048]{1,0:T(8,128)(2,1)}, bf16[256,2048]{1,0:T(8,128)(2,1)S(1)}, u32[]{:S(2)}, u32[]{:S(2)}) %collective-permute-start.1) | collective-permute-done | bytes 1048608 | tf_op jit(solution)/shard_map/ppermute | solution.py:122
  26.4 1.7 collective-permute-start.2
  29.4 1.6 collective-permute-start.17
  31.1 2.7 collective-permute-start.19
  34.6 20.0 %collective-permute-done.17.refs_1_ = bf16[512,512]{1,0:T(8,128)(2,1)} collective-permute-done((bf16[512,512]{1,0:T(8,128)(2,1)S(1)}, bf16[512,512]{1,0:T(8,128)(2,1)}, u32[]{:S(2)}, u32[]{:S(2)}) %collective-permute-start.17) | collective-permute-done | bytes 524320 | tf_op jit(solution)/shard_map/ppermute | solution.py:122
  54.6 1.5 collective-permute-done.2.refs_3_
  56.2 13.2 %collective-permute-done.19.refs_2_ = bf16[512,512]{1,0:T(8,128)(2,1)} collective-permute-done((bf16[512,512]{1,0:T(8,128)(2,1)S(1)}, bf16[512,512]{1,0:T(8,128)(2,1)}, u32[]{:S(2)}, u32[]{:S(2)}) %collective-permute-start.19) | collective-permute-done | bytes 524320 | tf_op jit(solution)/shard_map/ppermute | solution.py:122
  69.4 1.5 collective-permute-start.16
  70.9 10.6 %collective-permute-start.11 = (bf16[512,512]{1,0:T(8,128)(2,1)S(1)}, bf16[512,512]{1,0:T(8,128)(2,1)S(1)}, u32[]{:S(2)}, u32[]{:S(2)}) collective-permute-start(bf16[512,512]{1,0:T(8,128)(2,1)S(1)} %pad_maximum_fusion.1.refs_0_), channel_id=1, source_target_pairs={{0,4},{2,6},{4,0},{6,2},{1,5},{3,7},{5,1},{7,3},{8,12},{10,14},{12... | collective-permute-start | bytes 1572872 | tf_op jit(solution)/shard_map/ppermute | solution.py:122
  82.4 1.9 collective-permute-start.13
  84.3 32.2 %collective-permute-done.11.refs_2_ = bf16[512,512]{1,0:T(8,128)(2,1)S(1)} collective-permute-done((bf16[512,512]{1,0:T(8,128)(2,1)S(1)}, bf16[512,512]{1,0:T(8,128)(2,1)S(1)}, u32[]{:S(2)}, u32[]{:S(2)}) %collective-permute-start.11) | collective-permute-done | bytes 524320 | tf_op jit(solution)/shard_map/ppermute | solution.py:122
  116.6 1.6 collective-permute-start.18
  121.9 8.2 %set_together.1.source_ref = bf16[1024,4096]{1,0:T(8,128)(2,1)} custom-call(s32[7]{0:T(128)} %stack.89.place_ref, bf16[256,2048]{1,0:T(8,128)(2,1)} %refs_0_.1, bf16[256,2048]{1,0:T(8,128)(2,1)} %copy-done.8, bf16[256,2048]{1,0:T(8,128)(2,1)} %copy-done.6, bf16[256,2048]{1,0:T(8,128)(2,1)} %copy-done.9, bf16[256,2048]{1,0:T(8,128)(2,1)} %copy-done.7, ...), custom_call_target="tpu_custom_call" | custom-call | bytes 16777216 | tf_op jit(solution)/shard_map/set_together/pallas_call | solution.py:151
  130.1 5.8 %project.5.refs_4_ = f32[1024,512]{1,0:T(8,128)} custom-call(bf16[1024,4096]{1,0:T(8,128)(2,1)} %set_together.1.source_ref, bf16[512,512]{1,0:T(8,128)(2,1)} %copy-done.4, bf16[512,512]{1,0:T(8,128)(2,1)} %collective-permute-done.17.refs_1_, bf16[512,512]{1,0:T(8,128)(2,1)} %collective-permute-done.19.refs_2_, bf16[512,512]{1,0:T(8,128)(2,1)} %collective-permute-done.21.refs_3_), custom_call_target="tpu_custom_call" | custom-call | flops 2147483648 | bytes 6291456 | tf_op jit(solution)/shard_map/project/pallas_call | solution.py:228
  138.9 4.0 %collective-permute-done.20.refs_2_ = bf16[512,512]{1,0:T(8,128)(2,1)S(1)} collective-permute-done((bf16[512,512]{1,0:T(8,128)(2,1)}, bf16[512,512]{1,0:T(8,128)(2,1)S(1)}, u32[]{:S(2)}, u32[]{:S(2)}) %collective-permute-start.20) | collective-permute-done | bytes 524320 | tf_op jit(solution)/shard_map/ppermute | solution.py:122
  142.9 1.5 collective-permute-start.14
  144.4 9.8 %collective-permute-done.22.refs_3_ = bf16[512,512]{1,0:T(8,128)(2,1)} collective-permute-done((bf16[512,512]{1,0:T(8,128)(2,1)}, bf16[512,512]{1,0:T(8,128)(2,1)}, u32[]{:S(2)}, u32[]{:S(2)}) %collective-permute-start.22) | collective-permute-done | bytes 524320 | tf_op jit(solution)/shard_map/ppermute | solution.py:122
  154.2 5.8 %project.6.x_ref = bf16[1024,512]{1,0:T(8,128)(2,1)} custom-call(bf16[1024,4096]{1,0:T(8,128)(2,1)} %set_together.1.source_ref, bf16[512,512]{1,0:T(8,128)(2,1)} %copy-done.24, bf16[512,512]{1,0:T(8,128)(2,1)} %copy-done.25, bf16[512,512]{1,0:T(8,128)(2,1)} %copy-done.26, bf16[512,512]{1,0:T(8,128)(2,1)} %collective-permute-done.22.refs_3_, ...), custom_call_target="tpu_custom_call" | custom-call | flops 2147483648 | bytes 6291456 | tf_op jit(solution)/shard_map/project/pallas_call | solution.py:228
  160.1 11.2 %gates.1 = (f32[4,1024,128]{2,1,0:T(8,128)}, f32[4,1024,128]{2,1,0:T(8,128)}, f32[2,24,512]{2,1,0:T(8,128)}, f32[2,16,512]{2,1,0:T(8,128)}) custom-call(s32[7]{0:T(128)} %stack.89.place_ref, bf16[1024,512]{1,0:T(8,128)(2,1)} %project.6.x_ref, f32[16,2048]{1,0:T(8,128)} %stack.102.table_ref, bf16[8,256,256]{2,1,0:T(8,128)(2,1)} %decay_w.3, ...), custom_call_target="tpu_custom_call" | custom-call | flops 536870912 | bytes 5242880 | tf_op jit(solution)/shard_map/gates/pallas_call | solution.py:361
  171.3 2.1 collective-permute-start.23
  174.3 2.5 collective-permute-done.23
  176.8 1.6 collective-permute-start.24
  178.3 5.6 %project.4.refs_4_ = f32[1024,512]{1,0:T(8,128)} custom-call(bf16[1024,4096]{1,0:T(8,128)(2,1)} %set_together.1.source_ref, bf16[512,512]{1,0:T(8,128)(2,1)} %copy-done.3, bf16[512,512]{1,0:T(8,128)(2,1)} %collective-permute-done.9.refs_1_, bf16[512,512]{1,0:T(8,128)(2,1)} %copy-done.15, bf16[512,512]{1,0:T(8,128)(2,1)} %collective-permute-done.13.refs_3_), custom_call_target="tpu_custom_call" | custom-call | flops 2147483648 | bytes 6291456 | tf_op jit(solution)/shard_map/project/pallas_call | solution.py:228
  184.0 14.7 %collective-permute-done.24 = f32[2,2,16,512]{3,2,1,0:T(8,128)S(1)} collective-permute-done((f32[2,2,16,512]{3,2,1,0:T(8,128)S(1)}, f32[2,2,16,512]{3,2,1,0:T(8,128)S(1)}, u32[]{:S(2)}, u32[]{:S(2)}) %collective-permute-start.24) | collective-permute-done | bytes 131104 | tf_op jit(solution)/shard_map/ppermute | solution.py:122
  200.6 8.4 %states.1.refs_5_ = f32[4,1024,128]{2,1,0:T(8,128)} custom-call(s32[7]{0:T(128)} %stack.89.place_ref, f32[4,1024,128]{2,1,0:T(8,128)} %get-tuple-element.25.decay_ref, f32[4,1024,128]{2,1,0:T(8,128)} %get-tuple-element.26.drive_ref, f32[2,24,512]{2,1,0:T(8,128)} %get-tuple-element.27.part_ref, f32[8,16,512]{2,1,0:T(8,128)} %bitcast.39, ...), custom_call_target="tpu_custom_call" | custom-call | flops 5242880 | bytes 6291456 | tf_op jit(solution)/shard_map/states/pallas_call | solution.py:520
  211.0 6.6 %project.7.refs_0_ = bf16[1024,512]{1,0:T(8,128)(2,1)} custom-call(bf16[1024,4096]{1,0:T(8,128)(2,1)} %set_together.1.source_ref, bf16[512,512]{1,0:T(8,128)(2,1)} %copy-done.17, bf16[512,512]{1,0:T(8,128)(2,1)} %copy-done.18, bf16[512,512]{1,0:T(8,128)(2,1)} %copy-done.19, bf16[512,512]{1,0:T(8,128)(2,1)} %copy-done.20, f32[1024,512]{1,0:T(8,128)} %project.4.refs_4_, ...), custom_call_target="tpu_custom_call" | custom-call | flops 2147483648 | bytes 6291456 | tf_op jit(solution)/shard_map/project/pallas_call | solution.py:228
  218.1 2.0 collective-permute-start.36
  220.1 1.5 collective-permute-start.27
  223.4 20.9 %collective-permute-done.36 = bf16[1024,256]{1,0:T(8,128)(2,1)S(1)} collective-permute-done((bf16[1024,256]{1,0:T(8,128)(2,1)S(1)}, bf16[1024,256]{1,0:T(8,128)(2,1)S(1)}, u32[]{:S(2)}, u32[]{:S(2)}) %collective-permute-start.36) | collective-permute-done | bytes 524320 | tf_op jit(solution)/shard_map/ppermute | solution.py:122
  245.8 2.0 broadcast_select_fusion.5
  248.8 2.3 broadcast_select_fusion
  251.0 8.0 %collective-permute-done.37 = bf16[1024,256]{1,0:T(8,128)(2,1)S(1)} collective-permute-done((bf16[1024,256]{1,0:T(8,128)(2,1)S(1)}, bf16[1024,256]{1,0:T(8,128)(2,1)S(1)}, u32[]{:S(2)}, u32[]{:S(2)}) %collective-permute-start.37) | collective-permute-done | bytes 524320 | tf_op jit(solution)/shard_map/ppermute | solution.py:122
  260.4 8.0 %collective-permute-done.30 = bf16[1024,256]{1,0:T(8,128)(2,1)S(1)} collective-permute-done((bf16[1024,256]{1,0:T(8,128)(2,1)S(1)}, bf16[1024,256]{1,0:T(8,128)(2,1)S(1)}, u32[]{:S(2)}, u32[]{:S(2)}) %collective-permute-start.30) | collective-permute-done | bytes 524320 | tf_op jit(solution)/shard_map/ppermute | solution.py:122
  269.8 1.5 collective-permute-start.31
  271.4 3.1 mix_near.5
  274.5 3.1 mix_near.4
  277.6 4.0 %mix_near.3 = f32[1024,512]{1,0:T(8,128)} custom-call(s32[7]{0:T(128)} %stack.89.place_ref, bf16[1024,512]{1,0:T(8,128)(2,1)} %project.7.refs_0_, bf16[1024,512]{1,0:T(8,128)(2,1)} %copy-done.2, bf16[1024,256]{1,0:T(8,128)(2,1)} %get-tuple-element.47.refs_2_, bf16[1024,256]{1,0:T(8,128)(2,1)} %get-tuple-element.45.refs_3_), custom_call_target="tpu_custom_call" | custom-call | flops 1073741824 | bytes 4194304 | tf_op jit(solution)/shard_map/mix_near/pallas_call | solution.py:560
  282.8 4.1 %mix_far.5 = (bf16[256,256]{1,0:T(8,128)(2,1)}, bf16[256,256]{1,0:T(8,128)(2,1)}, f32[256,256]{1,0:T(8,128)}, bf16[256,256]{1,0:T(8,128)(2,1)}) custom-call(s32[7]{0:T(128)} %stack.89.place_ref, bf16[2,2,256,512]{3,2,1,0:T(8,128)(2,1)} %bitcast.30, bf16[2,2,256,512]{3,2,1,0:T(8,128)(2,1)} %bitcast.33, bf16[1024,256]{1,0:T(8,128)(2,1)} %copy-done.22, ...), custom_call_target="tpu_custom_call" | custom-call | flops 536870912 | bytes 3932160 | tf_op jit(solution)/shard_map/mix_far/pallas_call | solution.py:627
  286.9 2.1 collective-permute-start.46
  289.0 4.1 %mix_far.4 = (bf16[256,256]{1,0:T(8,128)(2,1)}, bf16[256,256]{1,0:T(8,128)(2,1)}, f32[256,256]{1,0:T(8,128)}, bf16[256,256]{1,0:T(8,128)(2,1)}) custom-call(s32[7]{0:T(128)} %stack.89.place_ref, bf16[2,2,256,512]{3,2,1,0:T(8,128)(2,1)} %bitcast.31, bf16[2,2,256,512]{3,2,1,0:T(8,128)(2,1)} %bitcast.34, bf16[1024,256]{1,0:T(8,128)(2,1)} %copy-done.21, ...), custom_call_target="tpu_custom_call" | custom-call | flops 536870912 | bytes 3932160 | tf_op jit(solution)/shard_map/mix_far/pallas_call | solution.py:627
  293.9 1.8 collective-permute-done.31.refs_3_
  296.6 5.3 %mix_far.3 = (bf16[256,512]{1,0:T(8,128)(2,1)}, bf16[256,512]{1,0:T(8,128)(2,1)}, f32[256,512]{1,0:T(8,128)}, bf16[256,512]{1,0:T(8,128)(2,1)}) custom-call(s32[7]{0:T(128)} %stack.89.place_ref, bf16[2,2,256,512]{3,2,1,0:T(8,128)(2,1)} %bitcast.32, bf16[2,2,256,512]{3,2,1,0:T(8,128)(2,1)} %bitcast.35, bf16[1024,256]{1,0:T(8,128)(2,1)} %collective-permute-done.28.refs_2_, ...), custom_call_target="tpu_custom_call" | custom-call | flops 1073741824 | bytes 5767168 | tf_op jit(solution)/shard_map/mix_far/pallas_call | solution.py:627
  302.0 2.0 collective-permute-start.35
  305.6 14.1 %collective-permute-done.45.refs_9_ = bf16[256,256]{1,0:T(8,128)(2,1)S(1)} collective-permute-done((bf16[256,256]{1,0:T(8,128)(2,1)S(1)}, bf16[256,256]{1,0:T(8,128)(2,1)S(1)}, u32[]{:S(2)}, u32[]{:S(2)}) %collective-permute-start.45) | collective-permute-done | bytes 131104 | tf_op jit(solution)/shard_map/ppermute | solution.py:122
  320.7 2.8 place.1
  (172 shorter events, 30.4 us)
Async XLA Ops:
  0.0 26.4 %collective-permute-start.1 = (bf16[256,2048]{1,0:T(8,128)(2,1)}, bf16[256,2048]{1,0:T(8,128)(2,1)S(1)}, u32[]{:S(2)}, u32[]{:S(2)}) collective-permute-start(bf16[256,2048]{1,0:T(8,128)(2,1)} %refs_0_.1), channel_id=1, source_target_pairs={{0,2},{2,0},{4,6},{6,4},{1,3},{3,1},{5,7},{7,5},{8,10},{10,8},{12,... | collective-permute-start | bytes 3145736 | tf_op jit(solution)/shard_map/ppermute | solution.py:122
  6.4 21.8 %collective-permute-start.15 = (bf16[512,512]{1,0:T(8,128)(2,1)}, bf16[512,512]{1,0:T(8,128)(2,1)}, u32[]{:S(2)}, u32[]{:S(2)}) collective-permute-start(bf16[512,512]{1,0:T(8,128)(2,1)} %pad_maximum_fusion.3), channel_id=1, source_target_pairs={{0,8},{8,0},{16,24},{24,16},{1,9},{9,1},{17,25},{25,17},{2,10},{10... | collective-permute-start | bytes 1572872 | tf_op jit(solution)/shard_map/ppermute | solution.py:122
  8.0 25.7 %collective-permute-start.3 = (bf16[256,2048]{1,0:T(8,128)(2,1)S(1)}, bf16[256,2048]{1,0:T(8,128)(2,1)S(1)}, u32[]{:S(2)}, u32[]{:S(2)}) collective-permute-start(bf16[256,2048]{1,0:T(8,128)(2,1)S(1)} %copy-done.5), channel_id=1, source_target_pairs={{0,8},{8,0},{16,24},{24,16},{1,9},{9,1},{17,25},{25,17},{2,10},{10... | collective-permute-start | bytes 3145736 | tf_op jit(solution)/shard_map/ppermute | solution.py:122
  8.5 26.0 %collective-permute-start = (bf16[256,2048]{1,0:T(8,128)(2,1)S(1)}, bf16[256,2048]{1,0:T(8,128)(2,1)S(1)}, u32[]{:S(2)}, u32[]{:S(2)}) collective-permute-start(bf16[256,2048]{1,0:T(8,128)(2,1)S(1)} %copy-done.5), channel_id=1, source_target_pairs={{0,1},{1,0},{2,3},{3,2},{4,5},{5,4},{6,7},{7,6},{8,9},{9,8},{10,11... | collective-permute-start | bytes 3145736 | tf_op jit(solution)/shard_map/ppermute | solution.py:122
  26.4 29.7 %collective-permute-start.2 = (bf16[256,2048]{1,0:T(8,128)(2,1)S(1)}, bf16[256,2048]{1,0:T(8,128)(2,1)S(1)}, u32[]{:S(2)}, u32[]{:S(2)}) collective-permute-start(bf16[256,2048]{1,0:T(8,128)(2,1)S(1)} %collective-permute-done.1.refs_2_), channel_id=1, source_target_pairs={{0,1},{1,0},{2,3},{3,2},{4,5},{5,4},{6,7},{7,6},{8,9},{9,8},{10,11... | collective-permute-start | bytes 3145736 | tf_op jit(solution)/shard_map/ppermute | solution.py:122
  28.2 2.9 collective-permute-start.7
  29.4 25.2 %collective-permute-start.17 = (bf16[512,512]{1,0:T(8,128)(2,1)S(1)}, bf16[512,512]{1,0:T(8,128)(2,1)}, u32[]{:S(2)}, u32[]{:S(2)}) collective-permute-start(bf16[512,512]{1,0:T(8,128)(2,1)S(1)} %pad_maximum_fusion.5), channel_id=1, source_target_pairs={{0,2},{2,0},{4,6},{6,4},{1,3},{3,1},{5,7},{7,5},{8,10},{10,8},{12,... | collective-permute-start | bytes 1572872 | tf_op jit(solution)/shard_map/ppermute | solution.py:122
  31.1 38.4 %collective-permute-start.19 = (bf16[512,512]{1,0:T(8,128)(2,1)S(1)}, bf16[512,512]{1,0:T(8,128)(2,1)}, u32[]{:S(2)}, u32[]{:S(2)}) collective-permute-start(bf16[512,512]{1,0:T(8,128)(2,1)S(1)} %pad_maximum_fusion.4.refs_0_), channel_id=1, source_target_pairs={{0,4},{2,6},{4,0},{6,2},{1,5},{3,7},{5,1},{7,3},{8,12},{10,14},{12... | collective-permute-start | bytes 1572872 | tf_op jit(solution)/shard_map/ppermute | solution.py:122
  33.7 37.2 %collective-permute-start.21 = (bf16[512,512]{1,0:T(8,128)(2,1)S(1)}, bf16[512,512]{1,0:T(8,128)(2,1)}, u32[]{:S(2)}, u32[]{:S(2)}) collective-permute-start(bf16[512,512]{1,0:T(8,128)(2,1)S(1)} %pad_maximum_fusion.5), channel_id=1, source_target_pairs={{0,6},{2,4},{4,2},{6,0},{1,7},{3,5},{5,3},{7,1},{8,14},{10,12},{12... | collective-permute-start | bytes 1572872 | tf_op jit(solution)/shard_map/ppermute | solution.py:122
  34.6 82.0 %collective-permute-start.5 = (bf16[256,2048]{1,0:T(8,128)(2,1)S(1)}, bf16[256,2048]{1,0:T(8,128)(2,1)S(1)}, u32[]{:S(2)}, u32[]{:S(2)}) collective-permute-start(bf16[256,2048]{1,0:T(8,128)(2,1)S(1)} %collective-permute-done.1.refs_2_), channel_id=1, source_target_pairs={{0,8},{8,0},{16,24},{24,16},{1,9},{9,1},{17,25},{25,17},{2,10},{10... | collective-permute-start | bytes 3145736 | tf_op jit(solution)/shard_map/ppermute | solution.py:122
  54.6 63.6 %collective-permute-start.4 = (bf16[256,2048]{1,0:T(8,128)(2,1)S(1)}, bf16[256,2048]{1,0:T(8,128)(2,1)S(1)}, u32[]{:S(2)}, u32[]{:S(2)}) collective-permute-start(bf16[256,2048]{1,0:T(8,128)(2,1)S(1)} %collective-permute-done.refs_1_), channel_id=1, source_target_pairs={{0,8},{8,0},{16,24},{24,16},{1,9},{9,1},{17,25},{25,17},{2,10},{10... | collective-permute-start | bytes 3145736 | tf_op jit(solution)/shard_map/ppermute | solution.py:122
  56.1 62.7 %collective-permute-start.6 = (bf16[256,2048]{1,0:T(8,128)(2,1)S(1)}, bf16[256,2048]{1,0:T(8,128)(2,1)S(1)}, u32[]{:S(2)}, u32[]{:S(2)}) collective-permute-start(bf16[256,2048]{1,0:T(8,128)(2,1)S(1)} %collective-permute-done.2.refs_3_), channel_id=1, source_target_pairs={{0,8},{8,0},{16,24},{24,16},{1,9},{9,1},{17,25},{25,17},{2,10},{10... | collective-permute-start | bytes 3145736 | tf_op jit(solution)/shard_map/ppermute | solution.py:122
  69.4 13.0 %collective-permute-start.16 = (bf16[512,512]{1,0:T(8,128)(2,1)S(1)}, bf16[512,512]{1,0:T(8,128)(2,1)S(1)}, u32[]{:S(2)}, u32[]{:S(2)}) collective-permute-start(bf16[512,512]{1,0:T(8,128)(2,1)S(1)} %pad_maximum_fusion.4.refs_0_), channel_id=1, source_target_pairs={{0,16},{8,24},{16,0},{24,8},{1,17},{9,25},{17,1},{25,9},{2,18},{10... | collective-permute-start | bytes 1572872 | tf_op jit(solution)/shard_map/ppermute | solution.py:122
  70.9 45.6 %collective-permute-start.11 = (bf16[512,512]{1,0:T(8,128)(2,1)S(1)}, bf16[512,512]{1,0:T(8,128)(2,1)S(1)}, u32[]{:S(2)}, u32[]{:S(2)}) collective-permute-start(bf16[512,512]{1,0:T(8,128)(2,1)S(1)} %pad_maximum_fusion.1.refs_0_), channel_id=1, source_target_pairs={{0,4},{2,6},{4,0},{6,2},{1,5},{3,7},{5,1},{7,3},{8,12},{10,14},{12... | collective-permute-start | bytes 1572872 | tf_op jit(solution)/shard_map/ppermute | solution.py:122
  82.4 53.5 %collective-permute-start.13 = (bf16[512,512]{1,0:T(8,128)(2,1)}, bf16[512,512]{1,0:T(8,128)(2,1)}, u32[]{:S(2)}, u32[]{:S(2)}) collective-permute-start(bf16[512,512]{1,0:T(8,128)(2,1)} %pad_maximum_fusion.2), channel_id=1, source_target_pairs={{0,6},{2,4},{4,2},{6,0},{1,7},{3,5},{5,3},{7,1},{8,14},{10,12},{12... | collective-permute-start | bytes 1572872 | tf_op jit(solution)/shard_map/ppermute | solution.py:122
  116.6 20.3 %collective-permute-start.9 = (bf16[512,512]{1,0:T(8,128)(2,1)}, bf16[512,512]{1,0:T(8,128)(2,1)}, u32[]{:S(2)}, u32[]{:S(2)}) collective-permute-start(bf16[512,512]{1,0:T(8,128)(2,1)} %pad_maximum_fusion.2), channel_id=1, source_target_pairs={{0,2},{2,0},{4,6},{6,4},{1,3},{3,1},{5,7},{7,5},{8,10},{10,8},{12,... | collective-permute-start | bytes 1572872 | tf_op jit(solution)/shard_map/ppermute | solution.py:122
  116.6 21.4 %collective-permute-start.18 = (bf16[512,512]{1,0:T(8,128)(2,1)}, bf16[512,512]{1,0:T(8,128)(2,1)S(1)}, u32[]{:S(2)}, u32[]{:S(2)}) collective-permute-start(bf16[512,512]{1,0:T(8,128)(2,1)} %collective-permute-done.17.refs_1_), channel_id=1, source_target_pairs={{0,16},{8,24},{16,0},{24,8},{1,17},{9,25},{17,1},{25,9},{2,18},{10... | collective-permute-start | bytes 1572872 | tf_op jit(solution)/shard_map/ppermute | solution.py:122
  118.2 24.7 %collective-permute-start.20 = (bf16[512,512]{1,0:T(8,128)(2,1)}, bf16[512,512]{1,0:T(8,128)(2,1)S(1)}, u32[]{:S(2)}, u32[]{:S(2)}) collective-permute-start(bf16[512,512]{1,0:T(8,128)(2,1)} %collective-permute-done.19.refs_2_), channel_id=1, source_target_pairs={{0,16},{8,24},{16,0},{24,8},{1,17},{9,25},{17,1},{25,9},{2,18},{10... | collective-permute-start | bytes 1572872 | tf_op jit(solution)/shard_map/ppermute | solution.py:122
  120.1 34.1 %collective-permute-start.22 = (bf16[512,512]{1,0:T(8,128)(2,1)}, bf16[512,512]{1,0:T(8,128)(2,1)}, u32[]{:S(2)}, u32[]{:S(2)}) collective-permute-start(bf16[512,512]{1,0:T(8,128)(2,1)} %collective-permute-done.21.refs_3_), channel_id=1, source_target_pairs={{0,16},{8,24},{16,0},{24,8},{1,17},{9,25},{17,1},{25,9},{2,18},{10... | collective-permute-start | bytes 1572872 | tf_op jit(solution)/shard_map/ppermute | solution.py:122
  135.9 73.1 %collective-permute-start.8 = (bf16[512,512]{1,0:T(8,128)(2,1)S(1)}, bf16[512,512]{1,0:T(8,128)(2,1)S(1)}, u32[]{:S(2)}, u32[]{:S(2)}) collective-permute-start(bf16[512,512]{1,0:T(8,128)(2,1)S(1)} %pad_maximum_fusion.1.refs_0_), channel_id=1, source_target_pairs={{0,16},{8,24},{16,0},{24,8},{1,17},{9,25},{17,1},{25,9},{2,18},{10... | collective-permute-start | bytes 1572872 | tf_op jit(solution)/shard_map/ppermute | solution.py:122
  136.9 72.2 %collective-permute-start.10 = (bf16[512,512]{1,0:T(8,128)(2,1)}, bf16[512,512]{1,0:T(8,128)(2,1)S(1)}, u32[]{:S(2)}, u32[]{:S(2)}) collective-permute-start(bf16[512,512]{1,0:T(8,128)(2,1)} %collective-permute-done.9.refs_1_), channel_id=1, source_target_pairs={{0,16},{8,24},{16,0},{24,8},{1,17},{9,25},{17,1},{25,9},{2,18},{10... | collective-permute-start | bytes 1572872 | tf_op jit(solution)/shard_map/ppermute | solution.py:122
  138.0 71.1 %collective-permute-start.12 = (bf16[512,512]{1,0:T(8,128)(2,1)S(1)}, bf16[512,512]{1,0:T(8,128)(2,1)S(1)}, u32[]{:S(2)}, u32[]{:S(2)}) collective-permute-start(bf16[512,512]{1,0:T(8,128)(2,1)S(1)} %copy-done.16), channel_id=1, source_target_pairs={{0,16},{8,24},{16,0},{24,8},{1,17},{9,25},{17,1},{25,9},{2,18},{10... | collective-permute-start | bytes 1572872 | tf_op jit(solution)/shard_map/ppermute | solution.py:122
  142.9 66.2 %collective-permute-start.14 = (bf16[512,512]{1,0:T(8,128)(2,1)}, bf16[512,512]{1,0:T(8,128)(2,1)S(1)}, u32[]{:S(2)}, u32[]{:S(2)}) collective-permute-start(bf16[512,512]{1,0:T(8,128)(2,1)} %collective-permute-done.13.refs_3_), channel_id=1, source_target_pairs={{0,16},{8,24},{16,0},{24,8},{1,17},{9,25},{17,1},{25,9},{2,18},{10... | collective-permute-start | bytes 1572872 | tf_op jit(solution)/shard_map/ppermute | solution.py:122
  171.3 5.4 %collective-permute-start.23 = (f32[2,16,512]{2,1,0:T(8,128)}, f32[2,16,512]{2,1,0:T(8,128)S(1)}, u32[]{:S(2)}, u32[]{:S(2)}) collective-permute-start(f32[2,16,512]{2,1,0:T(8,128)} %get-tuple-element.28), channel_id=1, source_target_pairs={{0,4},{2,6},{4,0},{6,2},{1,5},{3,7},{5,1},{7,3},{8,12},{10,14},{12... | collective-permute-start | bytes 196616 | tf_op jit(solution)/shard_map/ppermute | solution.py:122
  176.8 21.9 %collective-permute-start.24 = (f32[2,2,16,512]{3,2,1,0:T(8,128)S(1)}, f32[2,2,16,512]{3,2,1,0:T(8,128)S(1)}, u32[]{:S(2)}, u32[]{:S(2)}) collective-permute-start(f32[2,2,16,512]{3,2,1,0:T(8,128)S(1)} %get-tuple-element.64), channel_id=1, source_target_pairs={{0,16},{8,24},{16,0},{24,8},{1,17},{9,25},{17,1},{25,9},{2,18},{10... | collective-permute-start | bytes 393224 | tf_op jit(solution)/shard_map/ppermute | solution.py:122
  198.7 24.1 %collective-permute-start.39 = (bf16[1024,256]{1,0:T(8,128)(2,1)}, bf16[1024,256]{1,0:T(8,128)(2,1)S(1)}, u32[]{:S(2)}, u32[]{:S(2)}) collective-permute-start(bf16[1024,256]{1,0:T(8,128)(2,1)} %get-tuple-element.49), channel_id=1, source_target_pairs={{0,6},{2,4},{4,2},{6,0},{1,7},{3,5},{5,3},{7,1},{8,14},{10,12},{12... | collective-permute-start | bytes 1572872 | tf_op jit(solution)/shard_map/ppermute | solution.py:122
  217.6 31.1 %collective-permute-start.25 = (bf16[1024,512]{1,0:T(8,128)(2,1)}, bf16[1024,512]{1,0:T(8,128)(2,1)S(1)}, u32[]{:S(2)}, u32[]{:S(2)}) collective-permute-start(bf16[1024,512]{1,0:T(8,128)(2,1)} %project.7.refs_0_), channel_id=1, source_target_pairs={{0,1},{1,0},{2,3},{3,2},{4,5},{5,4},{6,7},{7,6},{8,9},{9,8},{10,11... | collective-permute-start | bytes 3145736 | tf_op jit(solution)/shard_map/ppermute | solution.py:122
  218.1 26.1 %collective-permute-start.36 = (bf16[1024,256]{1,0:T(8,128)(2,1)S(1)}, bf16[1024,256]{1,0:T(8,128)(2,1)S(1)}, u32[]{:S(2)}, u32[]{:S(2)}) collective-permute-start(bf16[1024,256]{1,0:T(8,128)(2,1)S(1)} %get-tuple-element.50), channel_id=1, source_target_pairs={{0,4},{2,6},{4,0},{6,2},{1,5},{3,7},{5,1},{7,3},{8,12},{10,14},{12... | collective-permute-start | bytes 1572872 | tf_op jit(solution)/shard_map/ppermute | solution.py:122
  220.1 25.6 %collective-permute-start.27 = (bf16[1024,256]{1,0:T(8,128)(2,1)S(1)}, bf16[1024,256]{1,0:T(8,128)(2,1)}, u32[]{:S(2)}, u32[]{:S(2)}) collective-permute-start(bf16[1024,256]{1,0:T(8,128)(2,1)S(1)} %get-tuple-element.50), channel_id=1, source_target_pairs={{0,16},{8,24},{16,0},{24,8},{1,17},{9,25},{17,1},{25,9},{2,18},{10... | collective-permute-start | bytes 1572872 | tf_op jit(solution)/shard_map/ppermute | solution.py:122
  221.6 26.1 %collective-permute-start.29 = (bf16[1024,256]{1,0:T(8,128)(2,1)}, bf16[1024,256]{1,0:T(8,128)(2,1)S(1)}, u32[]{:S(2)}, u32[]{:S(2)}) collective-permute-start(bf16[1024,256]{1,0:T(8,128)(2,1)} %get-tuple-element.49), channel_id=1, source_target_pairs={{0,2},{2,0},{4,6},{6,4},{1,3},{3,1},{5,7},{7,5},{8,10},{10,8},{12,... | collective-permute-start | bytes 1572872 | tf_op jit(solution)/shard_map/ppermute | solution.py:122
  222.8 25.4 %collective-permute-start.40 = (bf16[1024,256]{1,0:T(8,128)(2,1)S(1)}, bf16[1024,256]{1,0:T(8,128)(2,1)}, u32[]{:S(2)}, u32[]{:S(2)}) collective-permute-start(bf16[1024,256]{1,0:T(8,128)(2,1)S(1)} %collective-permute-done.39), channel_id=1, source_target_pairs={{0,16},{8,24},{16,0},{24,8},{1,17},{9,25},{17,1},{25,9},{2,18},{10... | collective-permute-start | bytes 1572872 | tf_op jit(solution)/shard_map/ppermute | solution.py:122
  244.3 14.8 %collective-permute-start.37 = (bf16[1024,256]{1,0:T(8,128)(2,1)S(1)}, bf16[1024,256]{1,0:T(8,128)(2,1)S(1)}, u32[]{:S(2)}, u32[]{:S(2)}) collective-permute-start(bf16[1024,256]{1,0:T(8,128)(2,1)S(1)} %collective-permute-done.36), channel_id=1, source_target_pairs={{0,16},{8,24},{16,0},{24,8},{1,17},{9,25},{17,1},{25,9},{2,18},{10... | collective-permute-start | bytes 1572872 | tf_op jit(solution)/shard_map/ppermute | solution.py:122
  245.7 24.1 %collective-permute-start.32 = (bf16[1024,512]{1,0:T(8,128)(2,1)}, bf16[1024,512]{1,0:T(8,128)(2,1)S(1)}, u32[]{:S(2)}, u32[]{:S(2)}) collective-permute-start(bf16[1024,512]{1,0:T(8,128)(2,1)} %project.7.refs_0_), channel_id=1, source_target_pairs={{0,8},{8,0},{16,24},{24,16},{1,9},{9,1},{17,25},{25,17},{2,10},{10... | collective-permute-start | bytes 3145736 | tf_op jit(solution)/shard_map/ppermute | solution.py:122
  247.7 45.4 %collective-permute-start.28 = (bf16[1024,256]{1,0:T(8,128)(2,1)S(1)}, bf16[1024,256]{1,0:T(8,128)(2,1)}, u32[]{:S(2)}, u32[]{:S(2)}) collective-permute-start(bf16[1024,256]{1,0:T(8,128)(2,1)S(1)} %get-tuple-element.48), channel_id=1, source_target_pairs={{0,1},{1,0},{2,3},{3,2},{4,5},{5,4},{6,7},{7,6},{8,9},{9,8},{10,11... | collective-permute-start | bytes 1572872 | tf_op jit(solution)/shard_map/ppermute | solution.py:122
  248.2 20.2 %collective-permute-start.30 = (bf16[1024,256]{1,0:T(8,128)(2,1)S(1)}, bf16[1024,256]{1,0:T(8,128)(2,1)S(1)}, u32[]{:S(2)}, u32[]{:S(2)}) collective-permute-start(bf16[1024,256]{1,0:T(8,128)(2,1)S(1)} %collective-permute-done.29), channel_id=1, source_target_pairs={{0,16},{8,24},{16,0},{24,8},{1,17},{9,25},{17,1},{25,9},{2,18},{10... | collective-permute-start | bytes 1572872 | tf_op jit(solution)/shard_map/ppermute | solution.py:122
  248.7 32.9 %collective-permute-start.26 = (bf16[1024,512]{1,0:T(8,128)(2,1)S(1)}, bf16[1024,512]{1,0:T(8,128)(2,1)S(1)}, u32[]{:S(2)}, u32[]{:S(2)}) collective-permute-start(bf16[1024,512]{1,0:T(8,128)(2,1)S(1)} %collective-permute-done.25), channel_id=1, source_target_pairs={{0,8},{8,0},{16,24},{24,16},{1,9},{9,1},{17,25},{25,17},{2,10},{10... | collective-permute-start | bytes 3145736 | tf_op jit(solution)/shard_map/ppermute | solution.py:122
  259.0 22.6 %collective-permute-start.41 = (bf16[1024,256]{1,0:T(8,128)(2,1)S(1)}, bf16[1024,256]{1,0:T(8,128)(2,1)S(1)}, u32[]{:S(2)}, u32[]{:S(2)}) collective-permute-start(bf16[1024,256]{1,0:T(8,128)(2,1)S(1)} %get-tuple-element.42), channel_id=1, source_target_pairs={{0,1},{1,0},{2,3},{3,2},{4,5},{5,4},{6,7},{7,6},{8,9},{9,8},{10,11... | collective-permute-start | bytes 1572872 | tf_op jit(solution)/shard_map/ppermute | solution.py:122
  268.4 18.5 %collective-permute-start.38 = (bf16[1024,256]{1,0:T(8,128)(2,1)S(1)}, bf16[1024,256]{1,0:T(8,128)(2,1)S(1)}, u32[]{:S(2)}, u32[]{:S(2)}) collective-permute-start(bf16[1024,256]{1,0:T(8,128)(2,1)S(1)} %get-tuple-element.44), channel_id=1, source_target_pairs={{0,1},{1,0},{2,3},{3,2},{4,5},{5,4},{6,7},{7,6},{8,9},{9,8},{10,11... | collective-permute-start | bytes 1572872 | tf_op jit(solution)/shard_map/ppermute | solution.py:122
  269.8 25.9 %collective-permute-start.31 = (bf16[1024,256]{1,0:T(8,128)(2,1)S(1)}, bf16[1024,256]{1,0:T(8,128)(2,1)S(1)}, u32[]{:S(2)}, u32[]{:S(2)}) collective-permute-start(bf16[1024,256]{1,0:T(8,128)(2,1)S(1)} %get-tuple-element.46), channel_id=1, source_target_pairs={{0,1},{1,0},{2,3},{3,2},{4,5},{5,4},{6,7},{7,6},{8,9},{9,8},{10,11... | collective-permute-start | bytes 1572872 | tf_op jit(solution)/shard_map/ppermute | solution.py:122
  286.9 15.1 %collective-permute-start.42 = (bf16[256,256]{1,0:T(8,128)(2,1)}, bf16[256,256]{1,0:T(8,128)(2,1)S(1)}, u32[]{:S(2)}, u32[]{:S(2)}) collective-permute-start(bf16[256,256]{1,0:T(8,128)(2,1)} %get-tuple-element.34), channel_id=1, source_target_pairs={{0,2},{2,0},{4,6},{6,4},{1,3},{3,1},{5,7},{7,5},{8,10},{10,8},{12,... | collective-permute-start | bytes 393224 | tf_op jit(solution)/shard_map/ppermute | solution.py:122
  286.9 15.2 %collective-permute-start.44 = (bf16[256,256]{1,0:T(8,128)(2,1)}, bf16[256,256]{1,0:T(8,128)(2,1)S(1)}, u32[]{:S(2)}, u32[]{:S(2)}) collective-permute-start(bf16[256,256]{1,0:T(8,128)(2,1)} %get-tuple-element.36), channel_id=1, source_target_pairs={{0,10},{2,8},{4,14},{6,12},{8,2},{10,0},{12,6},{14,4},{16,26},{18,... | collective-permute-start | bytes 393224 | tf_op jit(solution)/shard_map/ppermute | solution.py:786
  286.9 17.2 %collective-permute-start.46 = (bf16[256,256]{1,0:T(8,128)(2,1)}, bf16[256,256]{1,0:T(8,128)(2,1)S(1)}, u32[]{:S(2)}, u32[]{:S(2)}) collective-permute-start(bf16[256,256]{1,0:T(8,128)(2,1)} %get-tuple-element.39), channel_id=1, source_target_pairs={{0,8},{8,0},{16,24},{24,16},{1,9},{9,1},{17,25},{25,17},{2,10},{10... | collective-permute-start | bytes 393224 | tf_op jit(solution)/shard_map/ppermute | solution.py:122
  293.1 11.1 %collective-permute-start.43 = (bf16[256,256]{1,0:T(8,128)(2,1)}, bf16[256,256]{1,0:T(8,128)(2,1)S(1)}, u32[]{:S(2)}, u32[]{:S(2)}) collective-permute-start(bf16[256,256]{1,0:T(8,128)(2,1)} %get-tuple-element.35), channel_id=1, source_target_pairs={{0,8},{8,0},{16,24},{24,16},{1,9},{9,1},{17,25},{25,17},{2,10},{10... | collective-permute-start | bytes 393224 | tf_op jit(solution)/shard_map/ppermute | solution.py:122
  301.9 17.8 %collective-permute-start.33 = (bf16[256,512]{1,0:T(8,128)(2,1)}, bf16[256,512]{1,0:T(8,128)(2,1)S(1)}, u32[]{:S(2)}, u32[]{:S(2)}) collective-permute-start(bf16[256,512]{1,0:T(8,128)(2,1)} %get-tuple-element.30), channel_id=1, source_target_pairs={{0,2},{2,0},{4,6},{6,4},{1,3},{3,1},{5,7},{7,5},{8,10},{10,8},{12,... | collective-permute-start | bytes 786440 | tf_op jit(solution)/shard_map/ppermute | solution.py:122
  301.9 17.8 %collective-permute-start.34 = (bf16[256,512]{1,0:T(8,128)(2,1)}, bf16[256,512]{1,0:T(8,128)(2,1)S(1)}, u32[]{:S(2)}, u32[]{:S(2)}) collective-permute-start(bf16[256,512]{1,0:T(8,128)(2,1)} %get-tuple-element.31), channel_id=1, source_target_pairs={{0,8},{8,0},{16,24},{24,16},{1,9},{9,1},{17,25},{25,17},{2,10},{10... | collective-permute-start | bytes 786440 | tf_op jit(solution)/shard_map/ppermute | solution.py:122
  302.0 17.7 %collective-permute-start.35 = (bf16[256,512]{1,0:T(8,128)(2,1)}, bf16[256,512]{1,0:T(8,128)(2,1)S(1)}, u32[]{:S(2)}, u32[]{:S(2)}) collective-permute-start(bf16[256,512]{1,0:T(8,128)(2,1)} %get-tuple-element.32), channel_id=1, source_target_pairs={{0,10},{2,8},{4,14},{6,12},{8,2},{10,0},{12,6},{14,4},{16,26},{18,... | collective-permute-start | bytes 786440 | tf_op jit(solution)/shard_map/ppermute | solution.py:786
  304.1 15.6 %collective-permute-start.45 = (bf16[256,256]{1,0:T(8,128)(2,1)S(1)}, bf16[256,256]{1,0:T(8,128)(2,1)S(1)}, u32[]{:S(2)}, u32[]{:S(2)}) collective-permute-start(bf16[256,256]{1,0:T(8,128)(2,1)S(1)} %copy-done.44), channel_id=1, source_target_pairs={{0,2},{2,0},{4,6},{6,4},{1,3},{3,1},{5,7},{7,5},{8,10},{10,8},{12,... | collective-permute-start | bytes 393224 | tf_op jit(solution)/shard_map/ppermute | solution.py:122
  304.2 15.5 %collective-permute-start.47 = (bf16[256,256]{1,0:T(8,128)(2,1)S(1)}, bf16[256,256]{1,0:T(8,128)(2,1)S(1)}, u32[]{:S(2)}, u32[]{:S(2)}) collective-permute-start(bf16[256,256]{1,0:T(8,128)(2,1)S(1)} %copy-done.43), channel_id=1, source_target_pairs={{0,10},{2,8},{4,14},{6,12},{8,2},{10,0},{12,6},{14,4},{16,26},{18,... | collective-permute-start | bytes 393224 | tf_op jit(solution)/shard_map/ppermute | solution.py:786
  (45 other events, 677.3 us)
